TPU v7x, 32 devices: a whole 2x2x4 slice. The times are simulated.
32 devices in a mesh: groups: 2 (over x), ctx: 16 (over z, y, core).
Axes of the slice: x: 2, y: 2, z: 4, core: 2. Of those that a mesh axis runs over, the one named last changes fastest.
Arguments:
- mixer_input: bfloat16 [2048, 8192], P(('groups', 'ctx')), parts along dimension 0, may hold values from -6 to 6
- gate_input: bfloat16 [2048, 8192], P(('groups', 'ctx')), parts along dimension 0, may hold values from -6 to 6
- step_raw: bfloat16 [2048, 8192], P(('groups', 'ctx')), parts along dimension 0, may hold values from -4 to 4
- input_proj: float32 [2048, 16], P(('groups', 'ctx')), parts along dimension 0, may hold values from -0.6 to 0.6
- output_proj: float32 [2048, 16], P(('groups', 'ctx')), parts along dimension 0, may hold values from -1.8 to 1.8
- decay_log: float32 [8192, 16], replicated, may hold values from -12 to 0
- conv_weight: float32 [8192, 4], replicated, may hold values from -3 to 3
- conv_bias: float32 [8192], replicated, may hold values from -3 to 3
- skip_gain: float32 [8192], replicated, may hold values from 0.5 to 1.5
- query_heads: bfloat16 [2048, 4096], P(('groups', 'ctx')), parts along dimension 0, may hold values from -6 to 6
- key_heads: bfloat16 [2048, 512], P(('groups', 'ctx')), parts along dimension 0, may hold values from -4 to 4
- value_heads: bfloat16 [2048, 512], P(('groups', 'ctx')), parts along dimension 0, may hold values from -6 to 6
Outputs:
- mixer_output: bfloat16 [2048, 8192], P(('groups', 'ctx')), parts along dimension 0
- attention: bfloat16 [2048, 4096], P(('groups', 'ctx')), parts along dimension 0
There are 2 independent parts, one for each index of `groups`. A program takes and returns all parts, laid end to end along the dimension named above; an argument that names none is the same for every part. Nothing has to cross between parts.
All inputs are finite; a program needn't handle non-finite values.
Results may differ from a plain program's by a relative error of at most 0.0085.
Values may be sent and summed in bfloat16 or wider, within the bound.
A program may use at most 320 MiB of HBM per device.

v0:
```python
from functools import partial
import math

import jax
import jax.numpy as jnp
from jax import lax
from jax.sharding import PartitionSpec as P

STATE = 16
TAPS = 4
Q_HEADS = 32
KV_HEADS = 4
HEAD_DIM = 128


masked_floor = -1e30


def from_behind(shard, axis, by):
    size = lax.axis_size(axis)
    pairs = [(i, i + by) for i in range(size) if 0 <= i + by < size]
    return lax.ppermute(shard, axis, pairs)


def carried_in(shard, axis, join, neutral):
    place = lax.axis_index(axis)
    gathered = jax.tree.map(
        lambda a, kind: lax.all_gather(a.astype(kind), axis), shard, (jnp.bfloat16, jnp.bfloat16)
    )
    state = jax.tree.map(lambda a, e: jnp.zeros_like(a) + jnp.asarray(e, a.dtype), shard, neutral)

    def one(lap, state):
        return join(
            state,
            jax.tree.map(
                lambda a, own: lax.dynamic_index_in_dim(a, lap, 0, False).astype(own.dtype),
                gathered,
                shard,
            ),
        )

    return lax.fori_loop(0, place, one, state)


def local_block(hidden_state, token_block, decay_rates):
    step_now, inner_now, b_rows, c_rows = token_block
    outputs = []
    for position in range(step_now.shape[0]):
        decay_now = jnp.exp(step_now[position][None, :] * decay_rates)
        hidden_state = (
            decay_now * hidden_state
            + b_rows[position][:, None] * (step_now[position] * inner_now[position])[None, :]
        )
        outputs.append(jnp.sum(hidden_state * c_rows[position][:, None], axis=0))
    return (hidden_state, jnp.stack(outputs))


def carried_block(hidden_state, token_block, decay_rates):
    step_now, c_rows = token_block
    outputs = []
    for position in range(step_now.shape[0]):
        hidden_state = jnp.exp(step_now[position][None, :] * decay_rates) * hidden_state
        outputs.append(jnp.sum(hidden_state * c_rows[position][:, None], axis=0))
    return (hidden_state, jnp.stack(outputs))


def attend_rows(
    accumulated_total, key_piece, value_piece, first_row, queries4, query_places, score_scale
):
    key_rows = key_piece.shape[0]
    key_block = key_piece.reshape(key_rows, KV_HEADS, HEAD_DIM)
    value_block = value_piece.reshape(key_rows, KV_HEADS, HEAD_DIM)
    largest, totals, summed = accumulated_total
    scores = (
        jnp.einsum("tkgd,rkd->tkgr", queries4, key_block, preferred_element_type=jnp.float32)
        * score_scale
    )
    allowed = (first_row + jnp.arange(key_rows))[None, :] <= query_places[:, None]
    allowed = allowed[:, None, None, :]
    scores = jnp.where(allowed, scores, masked_floor)
    new_largest = jnp.maximum(largest, jnp.max(scores, axis=3))
    probs = jnp.where(allowed, jnp.exp(scores - new_largest[..., None]), 0.0)
    shrink = jnp.exp(largest - new_largest)
    totals = totals * shrink + jnp.sum(probs, axis=3)
    update = jnp.einsum(
        "tkgr,rkd->tkgd",
        probs.astype(jnp.bfloat16),
        value_block,
        preferred_element_type=jnp.float32,
    )
    summed = summed * shrink[..., None] + update
    return (new_largest, totals, summed)


def fold_keys(accumulated_total, pieces, queries4, query_places, score_scale):
    key_piece, value_piece = pieces
    key_rows = key_piece.shape[0]
    block_rows = math.gcd(key_rows, 512)
    block_count = key_rows // block_rows

    def one_step(step_index, inner_running):
        key_slab = lax.dynamic_slice_in_dim(key_piece, step_index * block_rows, block_rows, 0)
        value_slab = lax.dynamic_slice_in_dim(value_piece, step_index * block_rows, block_rows, 0)
        return attend_rows(
            inner_running,
            key_slab,
            value_slab,
            step_index * block_rows,
            queries4,
            query_places,
            score_scale,
        )

    return lax.fori_loop(0, block_count, one_step, accumulated_total)


def start_state_for(half_rows, groups_per):
    return (
        jnp.full((half_rows, KV_HEADS, groups_per), masked_floor, jnp.float32),
        jnp.zeros((half_rows, KV_HEADS, groups_per), jnp.float32),
        jnp.zeros((half_rows, KV_HEADS, groups_per, HEAD_DIM), jnp.float32),
    )


def finish_half(accumulated_total, half_rows):
    largest, totals, summed = accumulated_total
    return (summed / totals[..., None]).reshape(half_rows, Q_HEADS * HEAD_DIM).astype(jnp.bfloat16)


def per_device(
    mixer_input,
    gate_input,
    step_raw,
    input_proj,
    output_proj,
    decay_log,
    conv_weight,
    conv_bias,
    skip_gain,
    query_heads,
    key_heads,
    value_heads,
):
    rows_dev = mixer_input.shape[0]
    channels = mixer_input.shape[1]
    rim_rows = TAPS - 1
    rim = from_behind(mixer_input[rows_dev - rim_rows :], "ctx", 1)
    extended = jnp.concatenate([rim, mixer_input], axis=0)
    conv_sum = jnp.zeros((rows_dev, channels), jnp.float32) + conv_bias[None, :]
    for tap_index in range(TAPS):
        conv_sum = conv_sum + conv_weight[:, tap_index][None, :] * extended[
            tap_index : tap_index + rows_dev
        ].astype(jnp.float32)
    inner_act = jax.nn.silu(conv_sum)
    step_size = jax.nn.softplus(step_raw.astype(jnp.float32))
    decay_rates = jnp.transpose(-jnp.exp(decay_log))
    block_total = rows_dev // 8
    step_blocks = step_size.reshape(block_total, 8, channels)
    inner_blocks = inner_act.reshape(block_total, 8, channels)
    b_blocks = input_proj.reshape(block_total, 8, STATE)
    c_blocks = output_proj.reshape(block_total, 8, STATE)
    start_state = jnp.zeros((STATE, channels), jnp.float32)
    local_final, local_out = lax.scan(
        partial(local_block, decay_rates=decay_rates),
        start_state,
        (step_blocks, inner_blocks, b_blocks, c_blocks),
    )
    step_sum = jnp.sum(step_size, axis=0)
    decay_total = jnp.exp(decay_rates * step_sum[None, :])

    def join_decay(earlier, later):
        return (earlier[0] * later[0], later[0] * earlier[1] + later[1])

    entering = carried_in(
        (decay_total, local_final),
        "ctx",
        join_decay,
        (jnp.ones((STATE, channels), jnp.float32), start_state),
    )[1]
    carried_final, carried_out = lax.scan(
        partial(carried_block, decay_rates=decay_rates), entering, (step_blocks, c_blocks)
    )
    scan_out = (local_out + carried_out).reshape(rows_dev, channels)
    mixer_output = (
        (scan_out + skip_gain[None, :] * inner_act) * jax.nn.silu(gate_input.astype(jnp.float32))
    ).astype(jnp.bfloat16)
    groups_per = Q_HEADS // KV_HEADS
    score_scale = 1.0 / math.sqrt(HEAD_DIM)
    half_rows = rows_dev // 2
    own_index = lax.axis_index("ctx")
    first_place = own_index * rows_dev
    first_queries = query_heads[:half_rows]
    second_queries = query_heads[half_rows:]
    second_start = first_place + half_rows
    first_q4 = first_queries.reshape(half_rows, KV_HEADS, groups_per, HEAD_DIM)
    second_q4 = second_queries.reshape(half_rows, KV_HEADS, groups_per, HEAD_DIM)
    first_places = first_place + jnp.arange(half_rows)
    second_places = second_start + jnp.arange(half_rows)
    start_pair = (start_state_for(half_rows, groups_per), start_state_for(half_rows, groups_per))
    pieces = (
        lax.all_gather(key_heads, "ctx", axis=0, tiled=True),
        lax.all_gather(value_heads, "ctx", axis=0, tiled=True),
    )
    first_running = fold_keys(start_pair[0], pieces, first_q4, first_places, score_scale)
    latter_accumulated = fold_keys(start_pair[1], pieces, second_q4, second_places, score_scale)
    first_out = finish_half(first_running, half_rows)
    second_out = finish_half(latter_accumulated, half_rows)
    attention = jnp.concatenate([first_out, second_out], axis=0)
    return (mixer_output, attention)


def solution(mesh):
    in_specs = (
        P(("groups", "ctx"), None),
        P(("groups", "ctx"), None),
        P(("groups", "ctx"), None),
        P(("groups", "ctx"), None),
        P(("groups", "ctx"), None),
        P(),
        P(),
        P(),
        P(),
        P(("groups", "ctx"), None),
        P(("groups", "ctx"), None),
        P(("groups", "ctx"), None),
    )
    out_specs = (P(("groups", "ctx"), None), P(("groups", "ctx"), None))
    return jax.shard_map(
        per_device, mesh=mesh, in_specs=in_specs, out_specs=out_specs, check_vma=False
    )
```

profile of v0, /device:TPU:29, one launch (start us, length us, event | category | flops | bytes accessed | tf_op | source)
XLA Modules:
  0.0 268.1 jit_solution(12521998334596977041)
XLA Ops:
  10.9 3.9 %fusion.40 = (f32[8192]{0:T(1024)S(1)}, f32[8,8,8192]{2,1,0:T(8,128)}) fusion(bf16[64,8192]{1,0:T(8,128)(2,1)} %param.24), kind=kLoop, calls=%fused_computation.154 | loop fusion | flops 4186112 | bytes 3178496 | tf_op jit(solution)/shard_map/reduce_sum | solution.py:168
  18.6 3.4 %divide_multiply_fusion = f32[64,8192]{1,0:T(8,128)} fusion(bf16[64,8192]{1,0:T(8,128)(2,1)S(1)} %copy-done.2, bf16[3,8192]{1,0:T(4,128)(2,1)} %collective-permute-done, f32[8192]{0:T(1024)S(1)} %bitcast.386, f32[8192]{0:T(1024)S(1)} %bitcast.387, f32[8192]{0:T(1024)S(1)} %bitcast.385, f32[8192]{0:T(1024)S(1)} %bitcast.384, f32[8192]{0:T(1024)} %param.29), kind=kLoop, calls=%fused_computation.152 | loop fusion | flops 13107200 | bytes 3358720 | tf_op jit(solution)/shard_map/jit(silu)/mul | solution.py:154
  23.5 61.5 %while.75 = (s32[]{:T(128)}, f32[16,8192]{1,0:T(8,128)S(1)}, f32[8,8,8192]{2,1,0:T(8,128)}, f32[8,8,8192]{2,1,0:T(8,128)}, f32[16,8192]{1,0:T(8,128)S(1)}, /*ind...) while((s32[]{:T(128)}, f32[16,8192]{1,0:T(8,128)S(1)}, ...), condition=%wide.region_9.10_spmd.clone, body=%wide.region_0.9_spmd.clone.sunk | while | flops 9175050 | bytes 10295392 | solution.py:163
  23.5 3.1 %constant_dynamic-slice_fusion.40 = (f32[1,1,8192]{2,1,0:T(1,128)S(1)}, f32[1,1,8192]{2,1,0:T(1,128)S(1)}, f32[1,1,8192]{2,1,0:T(1,128)S(1)}, f32[1,1,8192]{2,1,...) fusion(f32[8,8,8192]{2,1,0:T(8,128)} %get-tuple-element.1120, ...), kind=kLoop, calls=%fused_computation.62.clone.1 | loop fusion | bytes 1048608 | tf_op jit(solution)/shard_map/while/body/eval_jaxpr/slice | solution.py:52
  30.9 3.5 %constant_dynamic-slice_fusion.40 = (f32[1,1,8192]{2,1,0:T(1,128)S(1)}, f32[1,1,8192]{2,1,0:T(1,128)S(1)}, f32[1,1,8192]{2,1,0:T(1,128)S(1)}, f32[1,1,8192]{2,1,...) fusion(f32[8,8,8192]{2,1,0:T(8,128)} %get-tuple-element.1120, ...), kind=kLoop, calls=%fused_computation.62.clone.1 | loop fusion | bytes 1048608 | tf_op jit(solution)/shard_map/while/body/eval_jaxpr/slice | solution.py:52
  38.6 3.4 %constant_dynamic-slice_fusion.40 = (f32[1,1,8192]{2,1,0:T(1,128)S(1)}, f32[1,1,8192]{2,1,0:T(1,128)S(1)}, f32[1,1,8192]{2,1,0:T(1,128)S(1)}, f32[1,1,8192]{2,1,...) fusion(f32[8,8,8192]{2,1,0:T(8,128)} %get-tuple-element.1120, ...), kind=kLoop, calls=%fused_computation.62.clone.1 | loop fusion | bytes 1048608 | tf_op jit(solution)/shard_map/while/body/eval_jaxpr/slice | solution.py:52
  46.3 3.5 %constant_dynamic-slice_fusion.40 = (f32[1,1,8192]{2,1,0:T(1,128)S(1)}, f32[1,1,8192]{2,1,0:T(1,128)S(1)}, f32[1,1,8192]{2,1,0:T(1,128)S(1)}, f32[1,1,8192]{2,1,...) fusion(f32[8,8,8192]{2,1,0:T(8,128)} %get-tuple-element.1120, ...), kind=kLoop, calls=%fused_computation.62.clone.1 | loop fusion | bytes 1048608 | tf_op jit(solution)/shard_map/while/body/eval_jaxpr/slice | solution.py:52
  54.1 3.4 %constant_dynamic-slice_fusion.40 = (f32[1,1,8192]{2,1,0:T(1,128)S(1)}, f32[1,1,8192]{2,1,0:T(1,128)S(1)}, f32[1,1,8192]{2,1,0:T(1,128)S(1)}, f32[1,1,8192]{2,1,...) fusion(f32[8,8,8192]{2,1,0:T(8,128)} %get-tuple-element.1120, ...), kind=kLoop, calls=%fused_computation.62.clone.1 | loop fusion | bytes 1048608 | tf_op jit(solution)/shard_map/while/body/eval_jaxpr/slice | solution.py:52
  61.7 3.2 %constant_dynamic-slice_fusion.40 = (f32[1,1,8192]{2,1,0:T(1,128)S(1)}, f32[1,1,8192]{2,1,0:T(1,128)S(1)}, f32[1,1,8192]{2,1,0:T(1,128)S(1)}, f32[1,1,8192]{2,1,...) fusion(f32[8,8,8192]{2,1,0:T(8,128)} %get-tuple-element.1120, ...), kind=kLoop, calls=%fused_computation.62.clone.1 | loop fusion | bytes 1048608 | tf_op jit(solution)/shard_map/while/body/eval_jaxpr/slice | solution.py:52
  69.1 3.5 %constant_dynamic-slice_fusion.40 = (f32[1,1,8192]{2,1,0:T(1,128)S(1)}, f32[1,1,8192]{2,1,0:T(1,128)S(1)}, f32[1,1,8192]{2,1,0:T(1,128)S(1)}, f32[1,1,8192]{2,1,...) fusion(f32[8,8,8192]{2,1,0:T(8,128)} %get-tuple-element.1120, ...), kind=kLoop, calls=%fused_computation.62.clone.1 | loop fusion | bytes 1048608 | tf_op jit(solution)/shard_map/while/body/eval_jaxpr/slice | solution.py:52
  76.9 3.9 %constant_dynamic-slice_fusion.40 = (f32[1,1,8192]{2,1,0:T(1,128)S(1)}, f32[1,1,8192]{2,1,0:T(1,128)S(1)}, f32[1,1,8192]{2,1,0:T(1,128)S(1)}, f32[1,1,8192]{2,1,...) fusion(f32[8,8,8192]{2,1,0:T(8,128)} %get-tuple-element.1120, ...), kind=kLoop, calls=%fused_computation.62.clone.1 | loop fusion | bytes 1048608 | tf_op jit(solution)/shard_map/while/body/eval_jaxpr/slice | solution.py:52
  90.3 9.1 %while.77 = (s32[]{:T(128)}, f32[32,4,8]{0,2,1:T(8,128)S(1)}, f32[32,4,8]{0,2,1:T(8,128)S(1)}, f32[32,4,8,128]{3,0,2,1:T(8,128)}, bf16[1024,512]{0,1:T(8,128)(2,...) while((s32[]{:T(128)}, f32[32,4,8]{0,2,1:T(8,128)S(1)}, ...), condition=%wide.region_30.31_spmd.clone, body=%wide.region_27.30_spmd.clone.sunk | while | flops 275666464 | bytes 16126479 | solution.py:114
  101.5 9.0 %while.76 = (s32[]{:T(128)}, f32[32,4,8]{0,2,1:T(8,128)S(1)}, f32[32,4,8]{0,2,1:T(8,128)S(1)}, f32[32,4,8,128]{3,0,2,1:T(8,128)}, bf16[1024,512]{0,1:T(8,128)(2,...) while((s32[]{:T(128)}, f32[32,4,8]{0,2,1:T(8,128)S(1)}, ...), condition=%wide.region_26.27_spmd.clone, body=%wide.region_23.26_spmd.clone.sunk | while | flops 275666464 | bytes 15077875 | solution.py:114
  113.9 23.9 %all-gather.11.cloned.1.call-done = bf16[256,8192]{1,0:T(8,128)(2,1)} async-done(((bf16[16,8192]{1,0:T(8,128)(2,1)}), bf16[256,8192]{1,0:T(8,128)(2,1)}) %all-gather.11.cloned.1.call-update) | async-done | bytes 4194320 | tf_op jit(solution)/shard_map/all_gather | solution.py:28
  137.8 51.1 %all-gather.13.cloned.1.call-done = bf16[256,8192]{1,0:T(8,128)(2,1)} async-done(((bf16[16,8192]{1,0:T(8,128)(2,1)}), bf16[256,8192]{1,0:T(8,128)(2,1)}) %all-gather.13.cloned.1.call-update) | async-done | bytes 4194320 | tf_op jit(solution)/shard_map/all_gather | solution.py:28
  188.9 19.0 %while.73 = (s32[]{:T(128)}, f32[16,8192]{1,0:T(8,128)S(1)}, s32[]{:T(128)}, bf16[16,16,8192]{2,1,0:T(8,128)(2,1)}, bf16[16,16,8192]{2,1,0:T(8,128)(2,1)}, /*index=5*/s32[]{:T(128)}, s32[]{:T(128)}, s32[]{:T(128)}) while((s32[]{:T(128)}, f32[16,8192]{1,0:T(8,128)S(1)}, s32[]{:T(128)}, bf16[16,16,8192]{2,1,0:T(8,128)(2,1)}, ...), condition=%wide.region_12.13_spmd, body=%wide.region_11.12_spmd.sunk | while | flops 524293 | bytes 1572987 | solution.py:42
  208.0 49.3 %while.74 = (s32[]{:T(128)}, f32[16,8192]{1,0:T(8,128)S(1)}, f32[8,8,8192]{2,1,0:T(8,128)S(1)}, f32[8,8,8192]{2,1,0:T(8,128)}, f32[16,8192]{1,0:T(8,128)S(1)}, /...) while((s32[]{:T(128)}, f32[16,8192]{1,0:T(8,128)S(1)}, ...), condition=%wide.region_22.23_spmd, body=%wide.region_13.22_spmd.sunk | while | flops 4128777 | bytes 3672841 | solution.py:180
  214.1 2.3 constant_dynamic-slice_fusion.38
  220.2 2.6 constant_dynamic-slice_fusion.38
  226.6 2.6 constant_dynamic-slice_fusion.38
  233.0 2.3 constant_dynamic-slice_fusion.38
  245.1 2.3 constant_dynamic-slice_fusion.38
  251.2 2.3 constant_dynamic-slice_fusion.38
  257.4 4.2 %fusion.39 = bf16[64,8192]{1,0:T(8,128)(2,1)} fusion(bf16[64,8192]{1,0:T(8,128)(2,1)} %param.23, f32[64,8192]{1,0:T(8,128)} %divide_multiply_fusion, f32[8,8,8192]{2,1,0:T(8,128)} %get-tuple-element.401, f32[8,8,8192]{2,1,0:T(8,128)S(1)} %get-tuple-element.404, f32[8192]{0:T(1024)} %param.30), kind=kLoop, calls=%fused_computation.153 | loop fusion | flops 5242880 | bytes 8421376 | tf_op jit(solution)/shard_map/convert_element_type | solution.py:186
  (311 shorter events, 123.6 us)
Async XLA Ops:
  7.2 7.7 %copy-start.1 = (f32[8192,16]{0,1:T(8,128)S(1)}, f32[8192,16]{0,1:T(8,128)}, u32[]{:S(2)}) copy-start(f32[8192,16]{0,1:T(8,128)} %param.27) | copy-start | bytes 1572868
  7.2 78.6 %all-gather.7.cloned.1.call-start = ((), (), s32[]{:S(2)}) async-start(), calls=%async_computation | async-start | bytes 1114112 | tf_op jit(solution)/shard_map/all_gather | solution.py:201
  7.9 80.2 %all-gather.9.cloned.1.call-start = ((), (), s32[]{:S(2)}) async-start(), calls=%async_computation.1 | async-start | bytes 1114112 | tf_op jit(solution)/shard_map/all_gather | solution.py:202
  9.5 9.0 %collective-permute-start = (bf16[3,8192]{1,0:T(4,128)(2,1)}, bf16[3,8192]{1,0:T(4,128)(2,1)}, u32[]{:S(2)}, u32[]{:S(2)}) collective-permute-start(bf16[3,8192]{1,0:T(4,128)(2,1)} %slice.231), channel_id=1, source_target_pairs={{0,1},{1,2},{2,3},{3,4},{4,5},{5,6},{6,7},{7,8},{8,9},{9,10},{10,1... | collective-permute-start | bytes 147464 | tf_op jit(solution)/shard_map/ppermute | solution.py:22
  10.8 5.0 %copy-start.10 = (f32[8192,4]{0,1:T(4,128)S(1)}, f32[8192,4]{0,1:T(4,128)}, u32[]{:S(2)}) copy-start(f32[8192,4]{0,1:T(4,128)} %param.28) | copy-start | bytes 393220
  10.9 5.7 %copy-start.3 = (bf16[64,4096]{1,0:T(8,128)(2,1)S(1)}, bf16[64,4096]{1,0:T(8,128)(2,1)}, u32[]{:S(2)}) copy-start(bf16[64,4096]{1,0:T(8,128)(2,1)} %param.31) | copy-start | bytes 1572868
  10.9 126.9 %all-gather.11.cloned.1.call-start = ((), (), s32[]{:S(2)}) async-start(), calls=%async_computation.2 | async-start | bytes 4456448 | tf_op jit(solution)/shard_map/all_gather | solution.py:28
  14.8 1.9 copy-start.11
  14.8 2.6 copy-start.12
  15.7 2.8 %copy-start.2 = (bf16[64,8192]{1,0:T(8,128)(2,1)S(1)}, bf16[64,8192]{1,0:T(8,128)(2,1)}, u32[]{:S(2)}) copy-start(bf16[64,8192]{1,0:T(8,128)(2,1)} %param.22) | copy-start | bytes 3145732
  15.7 173.2 %all-gather.13.cloned.1.call-start = ((), (), s32[]{:S(2)}) async-start(), calls=%async_computation.3 | async-start | bytes 4456448 | tf_op jit(solution)/shard_map/all_gather | solution.py:28
  16.6 1.9 copy-start.8
  16.6 1.9 copy-start.9
  90.3 1.4 copy-start
  92.3 1.0 copy-start.6
  94.1 0.8 copy-start.7
  94.9 1.4 copy-start
  96.8 1.1 copy-start.6
  98.7 0.8 copy-start.7
  103.4 1.1 copy-start.4
  105.3 0.8 copy-start.5
  107.9 1.0 copy-start.4
  109.7 0.8 copy-start.5
Sparse Core Ops, SparseCore 0:
  10.2 37.2 all-gather.6
  49.7 36.8 all-gather.8
  88.7 49.0 all-gather.10
  139.8 49.0 all-gather.12
where the time goes:
time: 270 us; the launch traced here: 268 us
  local copies, waits for them, and re-layouts  98.1 us (36%)
  waiting for transfers between devices  75.8 us (28%)
  other arithmetic  71.6 us (27%)
  between operations  14 us (5%)
  matrix products  5.07 us (2%)
    all_gather x2, waiting for transfers between devices, carried_in(): lax.all_gather(a.astype(kind), axis)  75 us
    slice x8, local copies, waits for them, and re-layouts, local_block(): inner_now[position]  27.5 us
    slice x8, local copies, waits for them, and re-layouts, carried_block(): step_now[position][None, :] * decay_rates  18.6 us
    add x15, other arithmetic, join_decay(): return (earlier[0] * later[0], later[0] * earlier[1] + later[1])  18.4 us
    reduce_sum x24, other arithmetic, local_block(): outputs.append(jnp.sum(hidden_state * c_rows[position][:, None], axis=0))  17.8 us
    reduce_sum x8, other arithmetic, carried_block(): outputs.append(jnp.sum(hidden_state * c_rows[position][:, None], axis=0))  15.3 us
    dynamic_slice x16, local copies, waits for them, and re-layouts, per_device(): lax.scan(partial(local_block, decay_rates=decay_rates), start_state, (ste...  11 us
    another operation x8, local copies, waits for them, and re-layouts, carried_block(): return (hidden_state, jnp.stack(outputs))  9.4 us
  transfers between devices with their start and end apart: 5, of which 2 were waited for; matrix products, arithmetic and copies ran while one was open for 37% of the time, Pallas kernels for 0%

commit v1 on v0

v1 whole, which is shorter than its diff:
```python
import math
from functools import partial

import jax
import jax.numpy as jnp
from jax import lax
from jax.experimental import pallas as pl
from jax.experimental.pallas import tpu as pltpu
from jax.sharding import PartitionSpec as P

STATE = 16
TAPS = 4
Q_HEADS = 32
KV_HEADS = 4
HEAD_DIM = 128
LANES = 128
SUB = 8
WIDE = SUB * LANES
MSG = 32
LOG2E = math.log2(math.e)


def silu(v):
    return v / (1.0 + jnp.exp(-v))


def first_pass(
    split, rim_ref, x_ref, raw_ref, w_ref, bias_ref, rate_ref, b_ref, step_ref, inner_ref, msg_ref, ext, fin
):
    rows = x_ref.shape[0]
    rim_rows = TAPS - 1
    ext[pl.ds(SUB - rim_rows, rim_rows), :] = rim_ref[...].astype(jnp.float32)
    ext[pl.ds(SUB, rows), :] = x_ref[...].astype(jnp.float32)
    for k in range(SUB):
        cols = pl.ds(k * LANES, LANES)
        conv = jnp.zeros((rows, LANES), jnp.float32) + bias_ref[:, cols]
        for tap in range(TAPS):
            conv = conv + w_ref[pl.ds(tap, 1), cols] * ext[pl.ds(SUB - rim_rows + tap, rows), cols]
        raw = raw_ref[:, cols].astype(jnp.float32)
        inner_ref[pl.ds(k, rows, stride=SUB), :] = silu(conv)
        step_ref[pl.ds(k, rows, stride=SUB), :] = jnp.maximum(raw, 0.0) + jnp.log1p(
            jnp.exp(-jnp.abs(raw))
        )
    rates = [rate_ref[pl.ds(n, SUB, stride=STATE), :] for n in range(STATE)]

    def one(t, carry):
        total, hs = carry
        step = step_ref[pl.ds(pl.multiple_of(t * SUB, SUB), SUB), :]
        u = step * inner_ref[pl.ds(pl.multiple_of(t * SUB, SUB), SUB), :]
        new = []
        for n in range(STATE):
            b = jnp.broadcast_to(b_ref[pl.ds(t * STATE + n, 1), :], (SUB, LANES))
            new.append(jnp.exp2(step * rates[n]) * hs[n] + u * b)
        return total + step, tuple(new)

    zero = jnp.zeros((SUB, LANES), jnp.float32)
    total, hs = lax.fori_loop(0, rows, one, (zero, (zero,) * STATE), unroll=2)
    per = STATE // split
    left = total
    pieces = []
    for n in range(per):
        piece = left.astype(jnp.bfloat16).astype(jnp.float32)
        pieces.append(piece)
        left = left - piece
    for part in range(split):
        for n in range(per):
            row = part * 2 * per + n
            fin[pl.ds(row, SUB, stride=MSG), :] = hs[part * per + n]
            fin[pl.ds(row + per, SUB, stride=MSG), :] = pieces[n]
    msg_ref[...] = fin[...].astype(jnp.bfloat16)


def join_pass(size, split, got_ref, rate_ref, ent_ref):
    per = STATE // split
    units = rate_ref.shape[0] // per
    for k in range(units):
        rate = rate_ref[pl.ds(k * per, per), :]
        h = jnp.zeros((per, LANES), jnp.float32)
        for d in range(size):
            ent_ref[pl.ds((d * units + k) * per, per), :] = h.astype(jnp.bfloat16)
            at = (d * units + k) * 2 * per
            own = got_ref[pl.ds(at, per), :].astype(jnp.float32)
            parts = got_ref[pl.ds(at + per, per), :].astype(jnp.float32)
            total = (parts[0:1] + parts[1:2]) + parts[2:3]
            h = jnp.exp2(rate * total) * h + own


def second_pass(
    step_ref, inner_ref, gate_ref, skip_ref, rate_ref, b_ref, c_ref, ent_ref, out_ref, ent, ysc
):
    rows = gate_ref.shape[0]
    ent[...] = ent_ref[...].astype(jnp.float32)
    rates = [rate_ref[pl.ds(n, SUB, stride=STATE), :] for n in range(STATE)]
    start = tuple(ent[pl.ds(n, SUB, stride=STATE), :] for n in range(STATE))
    skip = skip_ref[...]

    def one(t, hs):
        at = pl.ds(pl.multiple_of(t * SUB, SUB), SUB)
        step = step_ref[at, :]
        inner = inner_ref[at, :]
        u = step * inner
        sums = [skip * inner, None]
        new = []
        for n in range(STATE):
            row = pl.ds(t * STATE + n, 1)
            b = jnp.broadcast_to(b_ref[row, :], (SUB, LANES))
            c = jnp.broadcast_to(c_ref[row, :], (SUB, LANES))
            h = jnp.exp2(step * rates[n]) * hs[n] + u * b
            new.append(h)
            term = h * c
            sums[n % 2] = term if sums[n % 2] is None else sums[n % 2] + term
        ysc[at, :] = sums[0] + sums[1]
        return tuple(new)

    lax.fori_loop(0, rows, one, start, unroll=2)
    for k in range(SUB):
        cols = pl.ds(k * LANES, LANES)
        y = ysc[pl.ds(k, rows, stride=SUB), :]
        out_ref[:, cols] = (y * silu(gate_ref[:, cols].astype(jnp.float32))).astype(jnp.bfloat16)


def attend(place_ref, q_ref, k_ref, v_ref, out_ref):
    rows = q_ref.shape[0]
    keys = k_ref.shape[0]
    heads = q_ref.shape[1] // HEAD_DIM
    chunk = math.gcd(keys, 1024)
    scale = LOG2E / math.sqrt(HEAD_DIM)
    q = jnp.concatenate([q_ref[:, pl.ds(h * HEAD_DIM, HEAD_DIM)] for h in range(heads)], axis=0)

    def fold(first, running):
        at = pl.ds(first, chunk)
        scores = lax.dot_general(
            q, k_ref[at, :], (((1,), (1,)), ((), ())), preferred_element_type=jnp.float32
        ).reshape(heads, rows, chunk)
        place = place_ref[0] + lax.broadcasted_iota(jnp.int32, (1, rows, chunk), 1)
        allowed = first + lax.broadcasted_iota(jnp.int32, (1, rows, chunk), 2) <= place
        scores = jnp.where(allowed, scores, -1e30)
        largest = jnp.max(scores, axis=2, keepdims=True)
        if running is not None:
            largest = jnp.maximum(largest, running[0])
        probs = jnp.exp2((scores - largest) * scale)
        totals = jnp.sum(probs, axis=2, keepdims=True)
        summed = jnp.dot(
            probs.reshape(heads * rows, chunk).astype(jnp.bfloat16),
            v_ref[at, :],
            preferred_element_type=jnp.float32,
        ).reshape(heads, rows, HEAD_DIM)
        if running is not None:
            shrink = jnp.exp2((running[0] - largest) * scale)
            totals = totals + running[1] * shrink
            summed = summed + running[2] * shrink
        return largest, totals, summed

    running = fold(0, None)
    if keys > chunk:
        running = lax.fori_loop(
            1,
            keys // chunk,
            lambda i, held: fold(pl.multiple_of(i * chunk, chunk), held),
            running,
        )
    out = (running[2] / running[1]).astype(jnp.bfloat16)
    for h in range(heads):
        out_ref[:, pl.ds(h * HEAD_DIM, HEAD_DIM)] = out[h]


def full(shape):
    return pl.BlockSpec(shape, lambda *_: (0,) * len(shape))


def per_device(
    mixer_input,
    gate_input,
    step_raw,
    input_proj,
    output_proj,
    decay_log,
    conv_weight,
    conv_bias,
    skip_gain,
    query_heads,
    key_heads,
    value_heads,
):
    rows, channels = mixer_input.shape
    size = lax.axis_size("ctx")
    own = lax.axis_index("ctx")
    groups = channels // WIDE
    split = max(1, size // (channels // LANES))
    tiles = channels // LANES
    f32, bf16 = jnp.float32, jnp.bfloat16
    shape = jax.ShapeDtypeStruct

    rim = lax.ppermute(
        mixer_input[rows - (TAPS - 1) :], "ctx", [(i, i + 1) for i in range(size - 1)]
    )
    pairs = lax.all_gather(
        jnp.concatenate([key_heads, value_heads], axis=1), "ctx", axis=0, tiled=True
    )
    rates = -LOG2E * jnp.exp(decay_log)
    rates = rates.reshape(tiles, LANES, STATE).transpose(0, 2, 1).reshape(tiles * STATE, LANES)
    b_rows = jnp.broadcast_to(input_proj.reshape(-1, 1), (rows * STATE, LANES))
    c_rows = jnp.broadcast_to(output_proj.reshape(-1, 1), (rows * STATE, LANES))

    wide = pl.BlockSpec((rows, WIDE), lambda g: (0, g))
    slab = pl.BlockSpec((None, rows * SUB, LANES), lambda g: (g, 0, 0))
    rate_spec = pl.BlockSpec((SUB * STATE, LANES), lambda g: (g, 0))
    slab_shape = shape((groups, rows * SUB, LANES), f32)
    step, inner, message = pl.pallas_call(
        partial(first_pass, split),
        grid=(groups,),
        in_specs=[
            pl.BlockSpec((TAPS - 1, WIDE), lambda g: (0, g)),
            wide,
            wide,
            pl.BlockSpec((TAPS, WIDE), lambda g: (0, g)),
            pl.BlockSpec((1, WIDE), lambda g: (0, g)),
            rate_spec,
            full((rows * STATE, LANES)),
        ],
        out_specs=[slab, slab, pl.BlockSpec((SUB * MSG, LANES), lambda g: (g, 0))],
        out_shape=[slab_shape, slab_shape, shape((tiles * MSG, LANES), bf16)],
        scratch_shapes=[
            pltpu.VMEM((SUB + rows, WIDE), f32),
            pltpu.VMEM((SUB * MSG, LANES), f32),
        ],
        cost_estimate=pl.CostEstimate(
            flops=6 * rows * channels * STATE,
            bytes_accessed=8 * rows * channels,
            transcendentals=rows * channels * STATE,
        ),
        name="first_pass",
    )(rim, mixer_input, step_raw, conv_weight.T, conv_bias[None], rates, b_rows)

    got = lax.all_to_all(message, "ctx", 0, 0, tiled=True)
    share = tiles * STATE // size
    own_rates = lax.dynamic_slice_in_dim(rates, own * share, share, 0)
    answers = pl.pallas_call(
        partial(join_pass, size, split),
        out_shape=shape((tiles * STATE, LANES), bf16),
        name="join_pass",
    )(got, own_rates)
    entering = lax.all_to_all(answers, "ctx", 0, 0, tiled=True)

    panel = Q_HEADS // KV_HEADS * HEAD_DIM
    keys = rows * size
    attention = pl.pallas_call(
        attend,
        grid=(KV_HEADS,),
        in_specs=[
            pl.BlockSpec(memory_space=pltpu.SMEM),
            pl.BlockSpec((rows, panel), lambda g: (0, g)),
            pl.BlockSpec((keys, HEAD_DIM), lambda g: (0, g)),
            pl.BlockSpec((keys, HEAD_DIM), lambda g: (0, KV_HEADS + g)),
        ],
        out_specs=pl.BlockSpec((rows, panel), lambda g: (0, g)),
        out_shape=shape((rows, Q_HEADS * HEAD_DIM), bf16),
        cost_estimate=pl.CostEstimate(
            flops=4 * rows * Q_HEADS * keys * HEAD_DIM,
            bytes_accessed=4 * keys * KV_HEADS * HEAD_DIM,
            transcendentals=rows * Q_HEADS * keys,
        ),
        name="attend",
    )((own * rows).astype(jnp.int32)[None], query_heads, pairs, pairs)

    mixer_output = pl.pallas_call(
        second_pass,
        grid=(groups,),
        in_specs=[
            slab,
            slab,
            wide,
            pl.BlockSpec((SUB, LANES), lambda g: (g, 0)),
            rate_spec,
            full((rows * STATE, LANES)),
            full((rows * STATE, LANES)),
            rate_spec,
        ],
        out_specs=wide,
        out_shape=shape((rows, channels), bf16),
        scratch_shapes=[
            pltpu.VMEM((SUB * STATE, LANES), f32),
            pltpu.VMEM((rows * SUB, LANES), f32),
        ],
        cost_estimate=pl.CostEstimate(
            flops=8 * rows * channels * STATE,
            bytes_accessed=12 * rows * channels,
            transcendentals=rows * channels * STATE,
        ),
        name="second_pass",
    )(step, inner, gate_input, skip_gain.reshape(tiles, LANES), rates, b_rows, c_rows, entering)
    return (mixer_output, attention)


def solution(mesh):
    tokens = P(("groups", "ctx"), None)
    in_specs = (tokens,) * 5 + (P(),) * 4 + (tokens,) * 3
    return jax.shard_map(
        per_device, mesh=mesh, in_specs=in_specs, out_specs=(tokens, tokens), check_vma=False
    )
```

time: 270 us -> 107 us (0.40)
  the two profiles are of different devices: /device:TPU:29 before, /device:TPU:0 now
where the time goes in v1:
time: 107 us; the launch traced here: 106 us
  Pallas kernels  37.8 us (35%)
  waiting for transfers between devices  29.8 us (28%)
  starting transfers between devices  14.6 us (14%)
  between operations  14.1 us (13%)
  local copies, waits for them, and re-layouts  6.13 us (6%)
  other arithmetic  3.45 us (3%)
    all_to_all x1, waiting for transfers between devices, per_device(): got = lax.all_to_all(message, 'ctx', 0, 0, tiled=True)  19.9 us
    pallas_call x1, Pallas kernels, per_device(): pl.pallas_call(partial(first_pass, split), grid=(groups,), in_specs=[pl.B...  14.4 us
    pallas_call x1, Pallas kernels, per_device(): pl.pallas_call(second_pass, grid=(groups,), in_specs=[slab, slab, wide, p...  13.4 us
    all_to_all x1, waiting for transfers between devices, per_device(): entering = lax.all_to_all(answers, 'ctx', 0, 0, tiled=True)  9.87 us
    pallas_call x1, Pallas kernels, per_device(): pl.pallas_call(attend, grid=(KV_HEADS,), in_specs=[pl.BlockSpec(memory_sp...  8.03 us
    all_to_all x1, starting transfers between devices, per_device(): got = lax.all_to_all(message, 'ctx', 0, 0, tiled=True)  7.84 us
    all_to_all x1, starting transfers between devices, per_device(): entering = lax.all_to_all(answers, 'ctx', 0, 0, tiled=True)  4.36 us
    ppermute x1, starting transfers between devices, per_device(): lax.ppermute(mixer_input[rows - (TAPS - 1):], 'ctx', [(i, i + 1) for i in...  2.36 us
  transfers between devices with their start and end apart: 4, of which 2 were waited for; matrix products, arithmetic and copies ran while one was open for 7% of the time, Pallas kernels for 28%

profile of v1, /device:TPU:0, one launch (start us, length us, event | category | flops | bytes accessed | tf_op | source)
XLA Modules:
  0.0 105.8 jit_solution(10528252170953521746)
XLA Ops:
  7.2 0.0 all-gather.2.cloned.1.call-start
  7.2 1.5 %pad_maximum_fusion = bf16[64,1024]{1,0:T(8,128)(2,1)} fusion(bf16[64,512]{1,0:T(8,128)(2,1)} %param.23, bf16[64,512]{1,0:T(8,128)(2,1)} %param.22), kind=kLoop, calls=%fused_computation.2 | loop fusion | flops 262144 | bytes 262144 | tf_op jit(solution)/shard_map/concatenate | solution.py:198
  8.7 0.0 all-gather.2.cloned.1.call-update
  8.8 0.9 slice.3
  9.7 2.4 %collective-permute-start = (bf16[3,8192]{1,0:T(4,128)(2,1)S(1)}, bf16[3,8192]{1,0:T(4,128)(2,1)S(1)}, u32[]{:S(2)}, u32[]{:S(2)}) collective-permute-start(bf16[3,8192]{1,0:T(4,128)(2,1)S(1)} %slice.3), channel_id=1, source_target_pairs={{0,1},{1,2},{2,3},{3,4},{4,5},{5,6},{6,7},{7,8},{8,9},{9,10},{10,1... | collective-permute-start | bytes 147464 | tf_op jit(solution)/shard_map/ppermute | solution.py:194
  12.1 1.9 %copy_bitcast_fusion = f32[64,128,16]{1,2,0:T(8,128)} fusion(f32[8192,16]{0,1:T(8,128)} %param.17), kind=kLoop, calls=%fused_computation | loop fusion | flops 131072 | bytes 1048576 | tf_op jit(solution)/shard_map/reshape | solution.py:201
  14.0 0.8 copy.16
  14.8 0.1 broadcast_in_dim.21
  14.9 0.0 collective-permute-done.rim_ref
  14.9 1.0 broadcast_in_dim.22.b_ref
  15.9 14.4 %first_pass.1 = (f32[8,512,128]{2,1,0:T(8,128)}, f32[8,512,128]{2,1,0:T(8,128)}, bf16[2048,128]{1,0:T(8,128)(2,1)}) custom-call(bf16[3,8192]{1,0:T(4,128)(2,1)} %copy-done.3, bf16[64,8192]{1,0:T(8,128)(2,1)} %x_ref.1, bf16[64,8192]{1,0:T(8,128)(2,1)} %raw_ref.1, f32[4,8192]{1,0:T(4,128)} %bitcast.23, f32[1,8192]{1,0:T(1,128)} %bitcast.24, ...), custom_call_target="tpu_custom_call" | custom-call | flops 50331648 | bytes 4194304 | tf_op jit(solution)/shard_map/first_pass/pallas_call | solution.py:209
  30.3 7.8 %all-to-all-start = ((bf16[16,128,128]{2,1,0:T(8,128)(2,1)}), bf16[16,128,128]{2,1,0:T(8,128)(2,1)S(1)}, u32[]{:S(2)}, u32[]{:S(2)}) async-start(bf16[16,128,128]{2,1,0:T(8,128)(2,1)} %bitcast.21), calls=%async_computation | async-start | bytes 1048576 | tf_op jit(solution)/shard_map/all_to_all | solution.py:235
  38.1 1.4 %constant_dynamic-slice_fusion.rate_ref = f32[64,128]{1,0:T(8,128)} fusion(f32[1024,128]{1,0:T(8,128)} %bitcast.19, s32[]{:T(128)S(6)} %select_n.3), kind=kLoop, calls=%fused_computation.3 | loop fusion | bytes 65540 | tf_op jit(solution)/shard_map/dynamic_slice | solution.py:237
  39.5 19.9 %all-to-all-done = bf16[16,128,128]{2,1,0:T(8,128)(2,1)S(1)} async-done(((bf16[16,128,128]{2,1,0:T(8,128)(2,1)}), bf16[16,128,128]{2,1,0:T(8,128)(2,1)S(1)}, u32[]{:S(2)}, u32[]{:S(2)}) %all-to-all-start) | async-done | bytes 524320 | tf_op jit(solution)/shard_map/all_to_all | solution.py:235
  59.4 0.8 copy-done
  60.2 1.9 %join_pass.1 = bf16[1024,128]{1,0:T(8,128)(2,1)} custom-call(bf16[2048,128]{1,0:T(8,128)(2,1)} %bitcast.16, f32[64,128]{1,0:T(8,128)} %constant_dynamic-slice_fusion.rate_ref), custom_call_target="tpu_custom_call" | custom-call | tf_op jit(solution)/shard_map/join_pass/pallas_call | solution.py:238
  62.1 4.4 %all-to-all-start.1 = ((bf16[16,64,128]{2,1,0:T(8,128)(2,1)}), bf16[16,64,128]{2,1,0:T(8,128)(2,1)S(1)}, u32[]{:S(2)}, u32[]{:S(2)}) async-start(bf16[16,64,128]{2,1,0:T(8,128)(2,1)} %bitcast.17), calls=%async_computation.1 | async-start | bytes 524288 | tf_op jit(solution)/shard_map/all_to_all | solution.py:243
  66.5 0.1 copy.17
  66.6 0.1 broadcast_in_dim.23
  66.7 9.9 %all-to-all-done.1 = bf16[16,64,128]{2,1,0:T(8,128)(2,1)S(1)} async-done(((bf16[16,64,128]{2,1,0:T(8,128)(2,1)}), bf16[16,64,128]{2,1,0:T(8,128)(2,1)S(1)}, u32[]{:S(2)}, u32[]{:S(2)}) %all-to-all-start.1) | async-done | bytes 262176 | tf_op jit(solution)/shard_map/all_to_all | solution.py:243
  76.5 1.0 broadcast_in_dim.24.c_ref
  77.5 0.0 copy-done.1
  77.5 13.4 %second_pass.1 = bf16[64,8192]{1,0:T(8,128)(2,1)} custom-call(f32[8,512,128]{2,1,0:T(8,128)} %get-tuple-element.5.step_ref, f32[8,512,128]{2,1,0:T(8,128)} %get-tuple-element.6.inner_ref, bf16[64,8192]{1,0:T(8,128)(2,1)} %gate_ref.1, f32[64,128]{1,0:T(8,128)} %bitcast.25, f32[1024,128]{1,0:T(8,128)} %bitcast.20, f32[1024,128]{1,0:T(8,128)} %broadcast_in_dim.22.b_ref, ...), custom_call_target="tpu_custom_call" | custom-call | flops 67108864 | bytes 6291456 | tf_op jit(solution)/shard_map/second_pass/pallas_call | solution.py:266
  91.0 8.0 %attend.1 = bf16[64,4096]{1,0:T(8,128)(2,1)} custom-call(s32[1]{0:T(128)} %bitcast.10.place_ref, bf16[64,4096]{1,0:T(8,128)(2,1)} %q_ref.1, bf16[1024,1024]{1,0:T(8,128)(2,1)} %all-gather.2.cloned.1.call-done.k_ref.v_ref, bf16[1024,1024]{1,0:T(8,128)(2,1)} %all-gather.2.cloned.1.call-done.k_ref.v_ref), custom_call_target="tpu_custom_call" | custom-call | flops 1073741824 | bytes 2097152 | tf_op jit(solution)/shard_map/attend/pallas_call | solution.py:247
  (7 shorter events, 0.0 us)
Async XLA Ops:
  7.2 83.8 %all-gather.2.cloned.1.call-start = ((), (), s32[]{:S(2)}) async-start(), calls=%async_computation.2 | async-start | bytes 2228224 | tf_op jit(solution)/shard_map/all_gather | solution.py:197
  9.7 5.1 %collective-permute-start = (bf16[3,8192]{1,0:T(4,128)(2,1)S(1)}, bf16[3,8192]{1,0:T(4,128)(2,1)S(1)}, u32[]{:S(2)}, u32[]{:S(2)}) collective-permute-start(bf16[3,8192]{1,0:T(4,128)(2,1)S(1)} %slice.3), channel_id=1, source_target_pairs={{0,1},{1,2},{2,3},{3,4},{4,5},{5,6},{6,7},{7,8},{8,9},{9,10},{10,1... | collective-permute-start | bytes 147464 | tf_op jit(solution)/shard_map/ppermute | solution.py:194
  14.9 1.0 copy-start.3
  30.3 36.2 %copy-start.2 = (f32[64,16]{0,1:T(8,128)S(1)}, f32[64,16]{0,1:T(8,128)}, u32[]{:S(2)}) copy-start(f32[64,16]{0,1:T(8,128)} %param.16) | copy-start | bytes 12292
  30.3 29.1 %all-to-all-start = ((bf16[16,128,128]{2,1,0:T(8,128)(2,1)}), bf16[16,128,128]{2,1,0:T(8,128)(2,1)S(1)}, u32[]{:S(2)}, u32[]{:S(2)}) async-start(bf16[16,128,128]{2,1,0:T(8,128)(2,1)} %bitcast.21), calls=%async_computation | async-start | bytes 1048576 | tf_op jit(solution)/shard_map/all_to_all | solution.py:235
  59.4 0.8 copy-start
  62.1 14.4 %all-to-all-start.1 = ((bf16[16,64,128]{2,1,0:T(8,128)(2,1)}), bf16[16,64,128]{2,1,0:T(8,128)(2,1)S(1)}, u32[]{:S(2)}, u32[]{:S(2)}) async-start(bf16[16,64,128]{2,1,0:T(8,128)(2,1)} %bitcast.17), calls=%async_computation.1 | async-start | bytes 524288 | tf_op jit(solution)/shard_map/all_to_all | solution.py:243
  76.5 1.0 copy-start.1
Sparse Core Ops, SparseCore 0:
  10.2 50.1 all-gather.1

commit v2 on v1

--- a/solution.py
+++ b/solution.py
@@ -1,5 +1,4 @@
 import math
-from functools import partial
 
 import jax
 import jax.numpy as jnp
@@ -16,7 +15,7 @@
 LANES = 128
 SUB = 8
 WIDE = SUB * LANES
-MSG = 32
+HEAD = 16
 LOG2E = math.log2(math.e)
 
 
@@ -25,7 +24,8 @@
 
 
 def first_pass(
-    split, rim_ref, x_ref, raw_ref, w_ref, bias_ref, rate_ref, b_ref, step_ref, inner_ref, msg_ref, ext, fin
+    rim_ref, x_ref, raw_ref, w_ref, bias_ref, rate_ref, b_ref, step_ref, inner_ref, fin_ref, tot_ref,
+    ext, fin
 ):
     rows = x_ref.shape[0]
     rim_rows = TAPS - 1
@@ -55,34 +55,104 @@
 
     zero = jnp.zeros((SUB, LANES), jnp.float32)
     total, hs = lax.fori_loop(0, rows, one, (zero, (zero,) * STATE), unroll=2)
-    per = STATE // split
-    left = total
-    pieces = []
-    for n in range(per):
-        piece = left.astype(jnp.bfloat16).astype(jnp.float32)
-        pieces.append(piece)
-        left = left - piece
-    for part in range(split):
-        for n in range(per):
-            row = part * 2 * per + n
-            fin[pl.ds(row, SUB, stride=MSG), :] = hs[part * per + n]
-            fin[pl.ds(row + per, SUB, stride=MSG), :] = pieces[n]
-    msg_ref[...] = fin[...].astype(jnp.bfloat16)
-
-
-def join_pass(size, split, got_ref, rate_ref, ent_ref):
-    per = STATE // split
-    units = rate_ref.shape[0] // per
-    for k in range(units):
-        rate = rate_ref[pl.ds(k * per, per), :]
-        h = jnp.zeros((per, LANES), jnp.float32)
-        for d in range(size):
-            ent_ref[pl.ds((d * units + k) * per, per), :] = h.astype(jnp.bfloat16)
-            at = (d * units + k) * 2 * per
-            own = got_ref[pl.ds(at, per), :].astype(jnp.float32)
-            parts = got_ref[pl.ds(at + per, per), :].astype(jnp.float32)
-            total = (parts[0:1] + parts[1:2]) + parts[2:3]
-            h = jnp.exp2(rate * total) * h + own
+    for n in range(STATE):
+        fin[pl.ds(n, SUB, stride=STATE), :] = hs[n]
+    fin_ref[...] = fin[...].astype(jnp.bfloat16)
+    tot_ref[...] = total
+
+
+def exchange(
+    fin_ref, tot_ref, rate_ref, ent_ref, snd, got, ans, lands, send_a, recv_a, send_b, recv_b
+):
+    size, share, _ = ans.shape
+    tiles = tot_ref.shape[0]
+    count = max(1, tiles // size)
+    per = share // count
+    me = lax.axis_index("ctx")
+    barrier = pltpu.get_barrier_semaphore()
+
+    def greet(off, _):
+        pl.semaphore_signal(
+            barrier,
+            inc=1,
+            device_id={"ctx": lax.rem(me + off, size)},
+            device_id_type=pl.DeviceIdType.MESH,
+        )
+        return 0
+
+    lax.fori_loop(1, size, greet, 0)
+    filler = jnp.zeros((HEAD - 3 * count, LANES), jnp.float32)
+    for j in range(size):
+        left = tot_ref[pl.ds(j * tiles // size, count), :]
+        pieces = []
+        for _ in range(3):
+            pieces.append(left.astype(jnp.bfloat16).astype(jnp.float32))
+            left = left - pieces[-1]
+        snd[j, pl.ds(0, HEAD), :] = jnp.concatenate(pieces + [filler], axis=0).astype(jnp.bfloat16)
+        snd[j, pl.ds(HEAD, share), :] = fin_ref[pl.ds(j * share, share), :]
+    pl.semaphore_wait(barrier, size - 1)
+
+    def ask(to, origin):
+        return pltpu.make_async_remote_copy(
+            src_ref=snd.at[to],
+            dst_ref=got.at[origin],
+            send_sem=send_a.at[to],
+            recv_sem=recv_a.at[origin],
+            device_id={"ctx": to},
+            device_id_type=pl.DeviceIdType.MESH,
+        )
+
+    def answer(to, origin):
+        return pltpu.make_async_remote_copy(
+            src_ref=ans.at[to],
+            dst_ref=lands.at[origin],
+            send_sem=send_b.at[to],
+            recv_sem=recv_b.at[origin],
+            device_id={"ctx": to},
+            device_id_type=pl.DeviceIdType.MESH,
+        )
+
+    def start_ask(off, _):
+        ask(lax.rem(me + off, size), me).start()
+        return 0
+
+    lax.fori_loop(1, size, start_ask, 0)
+    got[me] = snd[me]
+
+    def join(d, hs):
+        @pl.when(d != me)
+        def _():
+            ask(d, d).wait_recv()
+
+        parts = got[d, pl.ds(0, HEAD), :].astype(jnp.float32)
+        new = []
+        for k in range(count):
+            ans[d, pl.ds(k * per, per), :] = hs[k].astype(jnp.bfloat16)
+            total = (
+                parts[k : k + 1] + parts[count + k : count + k + 1]
+            ) + parts[2 * count + k : 2 * count + k + 1]
+            rate = rate_ref[pl.ds(pl.multiple_of(me * share + k * per, SUB), per), :]
+            own = got[d, pl.ds(HEAD + k * per, per), :].astype(jnp.float32)
+            new.append(jnp.exp2(rate * total) * hs[k] + own)
+
+        @pl.when(d != me)
+        def _():
+            answer(d, me).start()
+
+        return tuple(new)
+
+    lax.fori_loop(0, size, join, (jnp.zeros((per, LANES), jnp.float32),) * count)
+    lands[me] = ans[me]
+
+    def finish(off, _):
+        other = lax.rem(me + off, size)
+        answer(other, other).wait_recv()
+        ask(other, other).wait_send()
+        answer(other, other).wait_send()
+        return 0
+
+    lax.fori_loop(1, size, finish, 0)
+    ent_ref[...] = lands[...]
 
 
 def second_pass(
@@ -186,7 +256,6 @@
     size = lax.axis_size("ctx")
     own = lax.axis_index("ctx")
     groups = channels // WIDE
-    split = max(1, size // (channels // LANES))
     tiles = channels // LANES
     f32, bf16 = jnp.float32, jnp.bfloat16
     shape = jax.ShapeDtypeStruct
@@ -206,8 +275,8 @@
     slab = pl.BlockSpec((None, rows * SUB, LANES), lambda g: (g, 0, 0))
     rate_spec = pl.BlockSpec((SUB * STATE, LANES), lambda g: (g, 0))
     slab_shape = shape((groups, rows * SUB, LANES), f32)
-    step, inner, message = pl.pallas_call(
-        partial(first_pass, split),
+    step, inner, finals, totals = pl.pallas_call(
+        first_pass,
         grid=(groups,),
         in_specs=[
             pl.BlockSpec((TAPS - 1, WIDE), lambda g: (0, g)),
@@ -218,11 +287,21 @@
             rate_spec,
             full((rows * STATE, LANES)),
         ],
-        out_specs=[slab, slab, pl.BlockSpec((SUB * MSG, LANES), lambda g: (g, 0))],
-        out_shape=[slab_shape, slab_shape, shape((tiles * MSG, LANES), bf16)],
+        out_specs=[
+            slab,
+            slab,
+            rate_spec,
+            pl.BlockSpec((SUB, LANES), lambda g: (g, 0)),
+        ],
+        out_shape=[
+            slab_shape,
+            slab_shape,
+            shape((tiles * STATE, LANES), bf16),
+            shape((tiles, LANES), f32),
+        ],
         scratch_shapes=[
             pltpu.VMEM((SUB + rows, WIDE), f32),
-            pltpu.VMEM((SUB * MSG, LANES), f32),
+            pltpu.VMEM((SUB * STATE, LANES), f32),
         ],
         cost_estimate=pl.CostEstimate(
             flops=6 * rows * channels * STATE,
@@ -232,15 +311,22 @@
         name="first_pass",
     )(rim, mixer_input, step_raw, conv_weight.T, conv_bias[None], rates, b_rows)
 
-    got = lax.all_to_all(message, "ctx", 0, 0, tiled=True)
     share = tiles * STATE // size
-    own_rates = lax.dynamic_slice_in_dim(rates, own * share, share, 0)
-    answers = pl.pallas_call(
-        partial(join_pass, size, split),
-        out_shape=shape((tiles * STATE, LANES), bf16),
-        name="join_pass",
-    )(got, own_rates)
-    entering = lax.all_to_all(answers, "ctx", 0, 0, tiled=True)
+    entering = pl.pallas_call(
+        exchange,
+        in_specs=[pl.BlockSpec(memory_space=pltpu.VMEM)] * 3,
+        out_specs=pl.BlockSpec(memory_space=pltpu.VMEM),
+        out_shape=shape((size, share, LANES), bf16),
+        scratch_shapes=[
+            pltpu.VMEM((size, HEAD + share, LANES), bf16),
+            pltpu.VMEM((size, HEAD + share, LANES), bf16),
+            pltpu.VMEM((size, share, LANES), bf16),
+            pltpu.VMEM((size, share, LANES), bf16),
+        ]
+        + [pltpu.SemaphoreType.DMA((size,))] * 4,
+        compiler_params=pltpu.CompilerParams(collective_id=0, has_side_effects=True),
+        name="exchange",
+    )(finals, totals, rates).reshape(tiles * STATE, LANES)
 
     panel = Q_HEADS // KV_HEADS * HEAD_DIM
     keys = rows * size

time: 107 us -> 89.5 us (0.84)
  waiting for transfers between devices: 29.8 us -> 0.02 us
  Pallas kernels: 37.8 us -> 63.6 us
  starting transfers between devices: 14.6 us -> 2.4 us
  local copies, waits for them, and re-layouts: 6.13 us -> 4.67 us
    all_to_all x2 -> x0, waiting for transfers between devices: 29.8 us -> none  [the longest x1 19.9 us: per_device(): got = lax.all_to_all(message, 'ctx', 0, 0, tiled=True)]
    pallas_call x2, Pallas kernels: 16.3 us -> 42.2 us  [the longest x1 28.3 us: per_device(): pl.pallas_call(exchange, in_specs=[pl.BlockSpec(memory_space=pltpu.VMEM)]...]
    all_to_all x2 -> x0, starting transfers between devices: 12.2 us -> none  [the longest x1 7.84 us: per_device(): got = lax.all_to_all(message, 'ctx', 0, 0, tiled=True)]
    dynamic_slice x1 -> x0, local copies, waits for them, and re-layouts: 1.38 us -> none  [per_device(): own_rates = lax.dynamic_slice_in_dim(rates, own * share, share, 0)]
  transfers between devices with their start and end apart: 4 -> 2, of which waited for: 2 -> 0; matrix products, arithmetic and copies ran while one was open for 7% -> 7% of each run, Pallas kernels for 28% -> 63%
where the time goes in v2:
time: 89.5 us; the launch traced here: 88.2 us
  Pallas kernels  63.6 us (71%)
  between operations  14.1 us (16%)
  local copies, waits for them, and re-layouts  4.67 us (5%)
  other arithmetic  3.43 us (4%)
  starting transfers between devices  2.4 us (3%)
    pallas_call x1, Pallas kernels, per_device(): pl.pallas_call(exchange, in_specs=[pl.BlockSpec(memory_space=pltpu.VMEM)]...  28.3 us
    pallas_call x1, Pallas kernels, per_device(): pl.pallas_call(first_pass, grid=(groups,), in_specs=[pl.BlockSpec((TAPS -...  13.9 us
    pallas_call x1, Pallas kernels, per_device(): pl.pallas_call(second_pass, grid=(groups,), in_specs=[slab, slab, wide, p...  13.4 us
    pallas_call x1, Pallas kernels, per_device(): pl.pallas_call(attend, grid=(KV_HEADS,), in_specs=[pl.BlockSpec(memory_sp...  8.03 us
    ppermute x1, starting transfers between devices, per_device(): lax.ppermute(mixer_input[rows - (TAPS - 1):], 'ctx', [(i, i + 1) for i in...  2.36 us
    reshape x1, other arithmetic, per_device(): rates.reshape(tiles, LANES, STATE).transpose(0, 2, 1)  1.91 us
  transfers between devices with their start and end apart: 2, of which 0 were waited for; matrix products, arithmetic and copies ran while one was open for 7% of the time, Pallas kernels for 63%

profile of v2, /device:TPU:0, one launch (start us, length us, event | category | flops | bytes accessed | tf_op | source)
XLA Modules:
  0.0 88.2 jit_solution(2093450120900197553)
XLA Ops:
  7.2 0.0 all-gather.2.cloned.1.call-start
  7.2 1.5 %pad_maximum_fusion = bf16[64,1024]{1,0:T(8,128)(2,1)} fusion(bf16[64,512]{1,0:T(8,128)(2,1)} %param.23, bf16[64,512]{1,0:T(8,128)(2,1)} %param.22), kind=kLoop, calls=%fused_computation.2 | loop fusion | flops 262144 | bytes 262144 | tf_op jit(solution)/shard_map/concatenate | solution.py:267
  8.7 0.0 all-gather.2.cloned.1.call-update
  8.8 0.9 %slice.3 = bf16[3,8192]{1,0:T(4,128)(2,1)S(1)} slice(bf16[64,8192]{1,0:T(8,128)(2,1)} %x_ref.1), slice={[61:64], [0:8192]} | slice | bytes 98304 | tf_op jit(solution)/shard_map/slice | solution.py:264
  9.7 2.4 %collective-permute-start = (bf16[3,8192]{1,0:T(4,128)(2,1)S(1)}, bf16[3,8192]{1,0:T(4,128)(2,1)S(1)}, u32[]{:S(2)}, u32[]{:S(2)}) collective-permute-start(bf16[3,8192]{1,0:T(4,128)(2,1)S(1)} %slice.3), channel_id=1, source_target_pairs={{0,1},{1,2},{2,3},{3,4},{4,5},{5,6},{6,7},{7,8},{8,9},{9,10},{10,1... | collective-permute-start | bytes 147464 | tf_op jit(solution)/shard_map/ppermute | solution.py:263
  12.1 1.9 %copy_bitcast_fusion = f32[64,128,16]{1,2,0:T(8,128)} fusion(f32[8192,16]{0,1:T(8,128)} %param.17), kind=kLoop, calls=%fused_computation | loop fusion | flops 131072 | bytes 1048576 | tf_op jit(solution)/shard_map/reshape | solution.py:270
  14.0 0.8 copy.16
  14.8 0.1 broadcast_in_dim.21
  14.8 0.8 copy.17
  15.6 0.1 broadcast_in_dim.23
  15.7 0.0 collective-permute-done.rim_ref
  15.7 0.0 copy-start
  15.7 1.0 %broadcast_in_dim.22.b_ref = f32[1024,128]{1,0:T(8,128)} broadcast(f32[1024]{0:T(1024)S(1)} %broadcast_in_dim.21), dimensions={0} | broadcast | bytes 528384 | tf_op jit(solution)/shard_map/broadcast_in_dim | solution.py:271
  16.7 0.0 copy-done
  16.7 13.9 %first_pass.1 = (f32[8,512,128]{2,1,0:T(8,128)}, f32[8,512,128]{2,1,0:T(8,128)}, bf16[1024,128]{1,0:T(8,128)(2,1)}, f32[64,128]{1,0:T(8,128)}) custom-call(bf16[3,8192]{1,0:T(4,128)(2,1)} %copy-done, bf16[64,8192]{1,0:T(8,128)(2,1)} %x_ref.1, bf16[64,8192]{1,0:T(8,128)(2,1)} %raw_ref.1, f32[4,8192]{1,0:T(4,128)} %bitcast.17, f32[1,8192]{1,0:T(1,128)} %bitcast.18, ...), custom_call_target="tpu_custom_call" | custom-call | flops 50331648 | bytes 4194304 | tf_op jit(solution)/shard_map/first_pass/pallas_call | solution.py:278
  30.6 28.3 %exchange.1 = bf16[16,64,128]{2,1,0:T(8,128)(2,1)} custom-call(bf16[1024,128]{1,0:T(8,128)(2,1)} %get-tuple-element.8.fin_ref, f32[64,128]{1,0:T(8,128)} %get-tuple-element.9.tot_ref, f32[1024,128]{1,0:T(8,128)} %bitcast.14), custom_call_target="tpu_custom_call" | custom-call | tf_op jit(solution)/shard_map/exchange/pallas_call | solution.py:315
  58.9 1.0 %broadcast_in_dim.24.c_ref = f32[1024,128]{1,0:T(8,128)} broadcast(f32[1024]{0:T(1024)S(1)} %broadcast_in_dim.23), dimensions={0} | broadcast | bytes 528384 | tf_op jit(solution)/shard_map/broadcast_in_dim | solution.py:272
  59.9 13.4 %second_pass.1 = bf16[64,8192]{1,0:T(8,128)(2,1)} custom-call(f32[8,512,128]{2,1,0:T(8,128)} %get-tuple-element.6.step_ref, f32[8,512,128]{2,1,0:T(8,128)} %get-tuple-element.7.inner_ref, bf16[64,8192]{1,0:T(8,128)(2,1)} %gate_ref.1, f32[64,128]{1,0:T(8,128)} %bitcast.19, f32[1024,128]{1,0:T(8,128)} %bitcast.15, f32[1024,128]{1,0:T(8,128)} %broadcast_in_dim.22.b_ref, ...), custom_call_target="tpu_custom_call" | custom-call | flops 67108864 | bytes 6291456 | tf_op jit(solution)/shard_map/second_pass/pallas_call | solution.py:352
  73.3 0.0 all-gather.2.cloned.1.call-done.k_ref.v_ref
  73.3 8.0 %attend.1 = bf16[64,4096]{1,0:T(8,128)(2,1)} custom-call(s32[1]{0:T(128)} %bitcast.7.place_ref, bf16[64,4096]{1,0:T(8,128)(2,1)} %q_ref.1, bf16[1024,1024]{1,0:T(8,128)(2,1)} %all-gather.2.cloned.1.call-done.k_ref.v_ref, bf16[1024,1024]{1,0:T(8,128)(2,1)} %all-gather.2.cloned.1.call-done.k_ref.v_ref), custom_call_target="tpu_custom_call" | custom-call | flops 1073741824 | bytes 2097152 | tf_op jit(solution)/shard_map/attend/pallas_call | solution.py:333
Async XLA Ops:
  7.2 66.2 %all-gather.2.cloned.1.call-start = ((), (), s32[]{:S(2)}) async-start(), calls=%async_computation | async-start | bytes 2228224 | tf_op jit(solution)/shard_map/all_gather | solution.py:266
  9.7 6.0 %collective-permute-start = (bf16[3,8192]{1,0:T(4,128)(2,1)S(1)}, bf16[3,8192]{1,0:T(4,128)(2,1)S(1)}, u32[]{:S(2)}, u32[]{:S(2)}) collective-permute-start(bf16[3,8192]{1,0:T(4,128)(2,1)S(1)} %slice.3), channel_id=1, source_target_pairs={{0,1},{1,2},{2,3},{3,4},{4,5},{5,6},{6,7},{7,8},{8,9},{9,10},{10,1... | collective-permute-start | bytes 147464 | tf_op jit(solution)/shard_map/ppermute | solution.py:263
  15.7 1.0 %copy-start = (bf16[3,8192]{1,0:T(4,128)(2,1)}, bf16[3,8192]{1,0:T(4,128)(2,1)S(1)}, u32[]{:S(2)}) copy-start(bf16[3,8192]{1,0:T(4,128)(2,1)S(1)} %collective-permute-done.rim_ref) | copy-start | bytes 147460
Sparse Core Ops, SparseCore 0:
  10.2 50.6 all-gather.1

commit v3 on v2

--- a/solution.py
+++ b/solution.py
@@ -24,9 +24,51 @@
 
 
 def first_pass(
-    rim_ref, x_ref, raw_ref, w_ref, bias_ref, rate_ref, b_ref, step_ref, inner_ref, fin_ref, tot_ref,
-    ext, fin
+    rim_ref, x_ref, raw_ref, w_ref, bias_ref, rate_ref, b_ref, all_rates_ref,
+    step_ref, inner_ref, ent_ref, ext, fin, snd, got, ans, lands, send_a, recv_a, send_b, recv_b
 ):
+    size, share, _ = ans.shape
+    group = pl.program_id(0)
+    groups = pl.num_programs(0)
+    share_count = STATE * SUB // share
+    count = max(1, SUB // share_count)
+    per = share // count
+    me = lax.axis_index("ctx")
+    barrier = pltpu.get_barrier_semaphore()
+
+    def greet(off, _):
+        pl.semaphore_signal(
+            barrier,
+            inc=1,
+            device_id={"ctx": lax.rem(me + off, size)},
+            device_id_type=pl.DeviceIdType.MESH,
+        )
+        return 0
+
+    @pl.when(group == 0)
+    def _():
+        lax.fori_loop(1, size, greet, 0)
+
+    def ask(to, origin):
+        return pltpu.make_async_remote_copy(
+            src_ref=snd.at[to],
+            dst_ref=got.at[origin],
+            send_sem=send_a.at[to],
+            recv_sem=recv_a.at[origin],
+            device_id={"ctx": to},
+            device_id_type=pl.DeviceIdType.MESH,
+        )
+
+    def answer(to, origin):
+        return pltpu.make_async_remote_copy(
+            src_ref=ans.at[to],
+            dst_ref=lands.at[origin],
+            send_sem=send_b.at[to],
+            recv_sem=recv_b.at[origin],
+            device_id={"ctx": to},
+            device_id_type=pl.DeviceIdType.MESH,
+        )
+
     rows = x_ref.shape[0]
     rim_rows = TAPS - 1
     ext[pl.ds(SUB - rim_rows, rim_rows), :] = rim_ref[...].astype(jnp.float32)
@@ -57,67 +99,26 @@
     total, hs = lax.fori_loop(0, rows, one, (zero, (zero,) * STATE), unroll=2)
     for n in range(STATE):
         fin[pl.ds(n, SUB, stride=STATE), :] = hs[n]
-    fin_ref[...] = fin[...].astype(jnp.bfloat16)
-    tot_ref[...] = total
-
-
-def exchange(
-    fin_ref, tot_ref, rate_ref, ent_ref, snd, got, ans, lands, send_a, recv_a, send_b, recv_b
-):
-    size, share, _ = ans.shape
-    tiles = tot_ref.shape[0]
-    count = max(1, tiles // size)
-    per = share // count
-    me = lax.axis_index("ctx")
-    barrier = pltpu.get_barrier_semaphore()
-
-    def greet(off, _):
-        pl.semaphore_signal(
-            barrier,
-            inc=1,
-            device_id={"ctx": lax.rem(me + off, size)},
-            device_id_type=pl.DeviceIdType.MESH,
-        )
-        return 0
-
-    lax.fori_loop(1, size, greet, 0)
+
+    @pl.when(group == 0)
+    def _():
+        pl.semaphore_wait(barrier, size - 1)
+
     filler = jnp.zeros((HEAD - 3 * count, LANES), jnp.float32)
-    for j in range(size):
-        left = tot_ref[pl.ds(j * tiles // size, count), :]
+    for part in range(share_count):
+        to = group * share_count + part
+        first = part * SUB // share_count
+        left = total[first : first + count]
         pieces = []
         for _ in range(3):
             pieces.append(left.astype(jnp.bfloat16).astype(jnp.float32))
             left = left - pieces[-1]
-        snd[j, pl.ds(0, HEAD), :] = jnp.concatenate(pieces + [filler], axis=0).astype(jnp.bfloat16)
-        snd[j, pl.ds(HEAD, share), :] = fin_ref[pl.ds(j * share, share), :]
-    pl.semaphore_wait(barrier, size - 1)
-
-    def ask(to, origin):
-        return pltpu.make_async_remote_copy(
-            src_ref=snd.at[to],
-            dst_ref=got.at[origin],
-            send_sem=send_a.at[to],
-            recv_sem=recv_a.at[origin],
-            device_id={"ctx": to},
-            device_id_type=pl.DeviceIdType.MESH,
-        )
-
-    def answer(to, origin):
-        return pltpu.make_async_remote_copy(
-            src_ref=ans.at[to],
-            dst_ref=lands.at[origin],
-            send_sem=send_b.at[to],
-            recv_sem=recv_b.at[origin],
-            device_id={"ctx": to},
-            device_id_type=pl.DeviceIdType.MESH,
-        )
-
-    def start_ask(off, _):
-        ask(lax.rem(me + off, size), me).start()
-        return 0
-
-    lax.fori_loop(1, size, start_ask, 0)
-    got[me] = snd[me]
+        snd[to, pl.ds(0, HEAD), :] = jnp.concatenate(pieces + [filler], axis=0).astype(jnp.bfloat16)
+        snd[to, pl.ds(HEAD, share), :] = fin[pl.ds(part * share, share), :].astype(jnp.bfloat16)
+
+        @pl.when(to != me)
+        def _():
+            ask(to, me).start()
 
     def join(d, hs):
         @pl.when(d != me)
@@ -131,7 +132,7 @@
             total = (
                 parts[k : k + 1] + parts[count + k : count + k + 1]
             ) + parts[2 * count + k : 2 * count + k + 1]
-            rate = rate_ref[pl.ds(pl.multiple_of(me * share + k * per, SUB), per), :]
+            rate = all_rates_ref[pl.ds(pl.multiple_of(me * share + k * per, SUB), per), :]
             own = got[d, pl.ds(HEAD + k * per, per), :].astype(jnp.float32)
             new.append(jnp.exp2(rate * total) * hs[k] + own)
 
@@ -141,8 +142,11 @@
 
         return tuple(new)
 
-    lax.fori_loop(0, size, join, (jnp.zeros((per, LANES), jnp.float32),) * count)
-    lands[me] = ans[me]
+    @pl.when(group == jnp.minimum(me // share_count + 2, groups - 1))
+    def _():
+        got[me] = snd[me]
+        lax.fori_loop(0, size, join, (jnp.zeros((per, LANES), jnp.float32),) * count)
+        lands[me] = ans[me]
 
     def finish(off, _):
         other = lax.rem(me + off, size)
@@ -151,8 +155,10 @@
         answer(other, other).wait_send()
         return 0
 
-    lax.fori_loop(1, size, finish, 0)
-    ent_ref[...] = lands[...]
+    @pl.when(group == groups - 1)
+    def _():
+        lax.fori_loop(1, size, finish, 0)
+        ent_ref[...] = lands[...]
 
 
 def second_pass(
@@ -234,10 +240,6 @@
         out_ref[:, pl.ds(h * HEAD_DIM, HEAD_DIM)] = out[h]
 
 
-def full(shape):
-    return pl.BlockSpec(shape, lambda *_: (0,) * len(shape))
-
-
 def per_device(
     mixer_input,
     gate_input,
@@ -268,14 +270,19 @@
     )
     rates = -LOG2E * jnp.exp(decay_log)
     rates = rates.reshape(tiles, LANES, STATE).transpose(0, 2, 1).reshape(tiles * STATE, LANES)
-    b_rows = jnp.broadcast_to(input_proj.reshape(-1, 1), (rows * STATE, LANES))
-    c_rows = jnp.broadcast_to(output_proj.reshape(-1, 1), (rows * STATE, LANES))
+    bc_rows = jnp.broadcast_to(
+        jnp.concatenate([input_proj, output_proj], axis=0).reshape(-1, 1),
+        (2 * rows * STATE, LANES),
+    )
+    b_spec = pl.BlockSpec((rows * STATE, LANES), lambda g: (0, 0))
+    c_spec = pl.BlockSpec((rows * STATE, LANES), lambda g: (1, 0))
+    share = tiles * STATE // size
 
     wide = pl.BlockSpec((rows, WIDE), lambda g: (0, g))
     slab = pl.BlockSpec((None, rows * SUB, LANES), lambda g: (g, 0, 0))
     rate_spec = pl.BlockSpec((SUB * STATE, LANES), lambda g: (g, 0))
     slab_shape = shape((groups, rows * SUB, LANES), f32)
-    step, inner, finals, totals = pl.pallas_call(
+    step, inner, entering = pl.pallas_call(
         first_pass,
         grid=(groups,),
         in_specs=[
@@ -285,39 +292,22 @@
             pl.BlockSpec((TAPS, WIDE), lambda g: (0, g)),
             pl.BlockSpec((1, WIDE), lambda g: (0, g)),
             rate_spec,
-            full((rows * STATE, LANES)),
+            b_spec,
+            pl.BlockSpec((tiles * STATE, LANES), lambda g: (0, 0)),
         ],
         out_specs=[
             slab,
             slab,
-            rate_spec,
-            pl.BlockSpec((SUB, LANES), lambda g: (g, 0)),
+            pl.BlockSpec((size, share, LANES), lambda g: (0, 0, 0)),
         ],
         out_shape=[
             slab_shape,
             slab_shape,
-            shape((tiles * STATE, LANES), bf16),
-            shape((tiles, LANES), f32),
+            shape((size, share, LANES), bf16),
         ],
         scratch_shapes=[
             pltpu.VMEM((SUB + rows, WIDE), f32),
             pltpu.VMEM((SUB * STATE, LANES), f32),
-        ],
-        cost_estimate=pl.CostEstimate(
-            flops=6 * rows * channels * STATE,
-            bytes_accessed=8 * rows * channels,
-            transcendentals=rows * channels * STATE,
-        ),
-        name="first_pass",
-    )(rim, mixer_input, step_raw, conv_weight.T, conv_bias[None], rates, b_rows)
-
-    share = tiles * STATE // size
-    entering = pl.pallas_call(
-        exchange,
-        in_specs=[pl.BlockSpec(memory_space=pltpu.VMEM)] * 3,
-        out_specs=pl.BlockSpec(memory_space=pltpu.VMEM),
-        out_shape=shape((size, share, LANES), bf16),
-        scratch_shapes=[
             pltpu.VMEM((size, HEAD + share, LANES), bf16),
             pltpu.VMEM((size, HEAD + share, LANES), bf16),
             pltpu.VMEM((size, share, LANES), bf16),
@@ -325,9 +315,15 @@
         ]
         + [pltpu.SemaphoreType.DMA((size,))] * 4,
         compiler_params=pltpu.CompilerParams(collective_id=0, has_side_effects=True),
-        name="exchange",
-    )(finals, totals, rates).reshape(tiles * STATE, LANES)
-
+        cost_estimate=pl.CostEstimate(
+            flops=6 * rows * channels * STATE,
+            bytes_accessed=8 * rows * channels,
+            transcendentals=rows * channels * STATE,
+        ),
+        name="first_pass",
+    )(rim, mixer_input, step_raw, conv_weight.T, conv_bias[None], rates, bc_rows, rates)
+
+    entering = entering.reshape(tiles * STATE, LANES)
     panel = Q_HEADS // KV_HEADS * HEAD_DIM
     keys = rows * size
     attention = pl.pallas_call(
@@ -358,8 +354,8 @@
             wide,
             pl.BlockSpec((SUB, LANES), lambda g: (g, 0)),
             rate_spec,
-            full((rows * STATE, LANES)),
-            full((rows * STATE, LANES)),
+            b_spec,
+            c_spec,
             rate_spec,
         ],
         out_specs=wide,
@@ -374,7 +370,7 @@
             transcendentals=rows * channels * STATE,
         ),
         name="second_pass",
-    )(step, inner, gate_input, skip_gain.reshape(tiles, LANES), rates, b_rows, c_rows, entering)
+    )(step, inner, gate_input, skip_gain.reshape(tiles, LANES), rates, bc_rows, bc_rows, entering)
     return (mixer_output, attention)
 
 

time: 89.5 us -> 88.1 us (0.984)
  the two profiles are of different devices: /device:TPU:0 before, /device:TPU:19 now
where the time goes in v3:
time: 88.1 us; the launch traced here: 87.8 us
  Pallas kernels  63.3 us (72%)
  between operations  14.1 us (16%)
  other arithmetic  4.22 us (5%)
  starting transfers between devices  3.75 us (4%)
  local copies, waits for them, and re-layouts  2.46 us (3%)
    pallas_call x1, Pallas kernels, per_device(): pl.pallas_call(first_pass, grid=(groups,), in_specs=[pl.BlockSpec((TAPS -...  41.8 us
    pallas_call x1, Pallas kernels, per_device(): pl.pallas_call(second_pass, grid=(groups,), in_specs=[slab, slab, wide, p...  13.4 us
    pallas_call x1, Pallas kernels, per_device(): pl.pallas_call(attend, grid=(KV_HEADS,), in_specs=[pl.BlockSpec(memory_sp...  8.03 us
    ppermute x1, starting transfers between devices, per_device(): lax.ppermute(mixer_input[rows - (TAPS - 1):], 'ctx', [(i, i + 1) for i in...  3.71 us
    reshape x1, other arithmetic, per_device(): rates.reshape(tiles, LANES, STATE).transpose(0, 2, 1)  1.91 us
  transfers between devices with their start and end apart: 2, of which 0 were waited for; matrix products, arithmetic and copies ran while one was open for 6% of the time, Pallas kernels for 63%

profile of v3, /device:TPU:19, one launch (start us, length us, event | category | flops | bytes accessed | tf_op | source)
XLA Modules:
  0.0 87.8 jit_solution(10151538601155062365)
XLA Ops:
  7.2 0.0 all-gather.2.cloned.1.call-start
  7.2 1.5 %pad_maximum_fusion = bf16[64,1024]{1,0:T(8,128)(2,1)} fusion(bf16[64,512]{1,0:T(8,128)(2,1)} %param.23, bf16[64,512]{1,0:T(8,128)(2,1)} %param.22), kind=kLoop, calls=%fused_computation.2 | loop fusion | flops 262144 | bytes 262144 | tf_op jit(solution)/shard_map/concatenate | solution.py:269
  8.7 0.0 all-gather.2.cloned.1.call-update
  8.8 0.9 %slice.3 = bf16[3,8192]{1,0:T(4,128)(2,1)S(1)} slice(bf16[64,8192]{1,0:T(8,128)(2,1)} %x_ref.1), slice={[61:64], [0:8192]} | slice | bytes 98304 | tf_op jit(solution)/shard_map/slice | solution.py:266
  9.7 3.7 %collective-permute-start = (bf16[3,8192]{1,0:T(4,128)(2,1)S(1)}, bf16[3,8192]{1,0:T(4,128)(2,1)S(1)}, u32[]{:S(2)}, u32[]{:S(2)}) collective-permute-start(bf16[3,8192]{1,0:T(4,128)(2,1)S(1)} %slice.3), channel_id=1, source_target_pairs={{0,1},{1,2},{2,3},{3,4},{4,5},{5,6},{6,7},{7,8},{8,9},{9,10},{10,1... | collective-permute-start | bytes 147464 | tf_op jit(solution)/shard_map/ppermute | solution.py:265
  13.4 1.9 %copy_bitcast_fusion = f32[64,128,16]{1,2,0:T(8,128)} fusion(f32[8192,16]{0,1:T(8,128)} %param.17), kind=kLoop, calls=%fused_computation | loop fusion | flops 131072 | bytes 1048576 | tf_op jit(solution)/shard_map/reshape | solution.py:272
  15.3 0.8 pad_maximum_fusion.1
  16.1 0.1 copy.16
  16.2 0.1 broadcast_in_dim.14
  16.3 0.0 collective-permute-done.rim_ref
  16.3 0.0 copy-start
  16.3 1.3 %broadcast_in_dim.15.b_ref.c_ref = f32[2048,128]{1,0:T(8,128)} broadcast(f32[2048]{0:T(1024)S(1)} %broadcast_in_dim.14), dimensions={0} | broadcast | bytes 1056768 | tf_op jit(solution)/shard_map/broadcast_in_dim | solution.py:273
  17.6 0.0 copy-done
  17.6 41.8 %first_pass.1 = (f32[8,512,128]{2,1,0:T(8,128)}, f32[8,512,128]{2,1,0:T(8,128)}, bf16[16,64,128]{2,1,0:T(8,128)(2,1)}) custom-call(bf16[3,8192]{1,0:T(4,128)(2,1)} %copy-done, bf16[64,8192]{1,0:T(8,128)(2,1)} %x_ref.1, bf16[64,8192]{1,0:T(8,128)(2,1)} %raw_ref.1, f32[4,8192]{1,0:T(4,128)} %bitcast.16, f32[1,8192]{1,0:T(1,128)} %bitcast.17, ...), custom_call_target="tpu_custom_call" | custom-call | flops 50331648 | bytes 4194304 | tf_op jit(solution)/shard_map/first_pass/pallas_call | solution.py:285
  59.4 13.4 %second_pass.1 = bf16[64,8192]{1,0:T(8,128)(2,1)} custom-call(f32[8,512,128]{2,1,0:T(8,128)} %get-tuple-element.5.step_ref, f32[8,512,128]{2,1,0:T(8,128)} %get-tuple-element.6.inner_ref, bf16[64,8192]{1,0:T(8,128)(2,1)} %gate_ref.1, f32[64,128]{1,0:T(8,128)} %bitcast.18, f32[1024,128]{1,0:T(8,128)} %bitcast.15, f32[2048,128]{1,0:T(8,128)} %broadcast_in_dim.15.b_ref.c_ref, ...), custom_call_target="tpu_custom_call" | custom-call | flops 67108864 | bytes 6291456 | tf_op jit(solution)/shard_map/second_pass/pallas_call | solution.py:348
  72.9 0.0 all-gather.2.cloned.1.call-done.k_ref.v_ref
  72.9 8.0 %attend.1 = bf16[64,4096]{1,0:T(8,128)(2,1)} custom-call(s32[1]{0:T(128)} %bitcast.6.place_ref, bf16[64,4096]{1,0:T(8,128)(2,1)} %q_ref.1, bf16[1024,1024]{1,0:T(8,128)(2,1)} %all-gather.2.cloned.1.call-done.k_ref.v_ref, bf16[1024,1024]{1,0:T(8,128)(2,1)} %all-gather.2.cloned.1.call-done.k_ref.v_ref), custom_call_target="tpu_custom_call" | custom-call | flops 1073741824 | bytes 2097152 | tf_op jit(solution)/shard_map/attend/pallas_call | solution.py:329
Async XLA Ops:
  7.2 65.7 %all-gather.2.cloned.1.call-start = ((), (), s32[]{:S(2)}) async-start(), calls=%async_computation | async-start | bytes 2228224 | tf_op jit(solution)/shard_map/all_gather | solution.py:268
  9.7 6.6 %collective-permute-start = (bf16[3,8192]{1,0:T(4,128)(2,1)S(1)}, bf16[3,8192]{1,0:T(4,128)(2,1)S(1)}, u32[]{:S(2)}, u32[]{:S(2)}) collective-permute-start(bf16[3,8192]{1,0:T(4,128)(2,1)S(1)} %slice.3), channel_id=1, source_target_pairs={{0,1},{1,2},{2,3},{3,4},{4,5},{5,6},{6,7},{7,8},{8,9},{9,10},{10,1... | collective-permute-start | bytes 147464 | tf_op jit(solution)/shard_map/ppermute | solution.py:265
  16.3 1.3 %copy-start = (bf16[3,8192]{1,0:T(4,128)(2,1)}, bf16[3,8192]{1,0:T(4,128)(2,1)S(1)}, u32[]{:S(2)}) copy-start(bf16[3,8192]{1,0:T(4,128)(2,1)S(1)} %collective-permute-done.rim_ref) | copy-start | bytes 147460
Sparse Core Ops, SparseCore 0:
  10.2 49.5 all-gather.1

commit v4 on v3

--- a/solution.py
+++ b/solution.py
@@ -2,6 +2,7 @@
 
 import jax
 import jax.numpy as jnp
+import numpy as np
 from jax import lax
 from jax.experimental import pallas as pl
 from jax.experimental.pallas import tpu as pltpu
@@ -25,7 +26,8 @@
 
 def first_pass(
     rim_ref, x_ref, raw_ref, w_ref, bias_ref, rate_ref, b_ref, all_rates_ref,
-    step_ref, inner_ref, ent_ref, ext, fin, snd, got, ans, lands, send_a, recv_a, send_b, recv_b
+    key_ref, value_ref, step_ref, inner_ref, ent_ref, pairs_ref,
+    ext, fin, snd, got, ans, lands, send_a, recv_a, send_b, recv_b, send_k, recv_k, own_k
 ):
     size, share, _ = ans.shape
     group = pl.program_id(0)
@@ -45,9 +47,35 @@
         )
         return 0
 
+    stages = size.bit_length() - 1
+    slot = sum(((me // 2**b) % 2) * 2 ** (stages - 1 - b) for b in range(stages))
+
+    def own_copies():
+        width = key_ref.shape[1]
+        return [
+            pltpu.make_async_copy(
+                source, pairs_ref.at[slot, :, pl.ds(i * width, width)], own_k.at[i]
+            )
+            for i, source in enumerate((key_ref, value_ref))
+        ]
+
+    def double(stage):
+        far = size // 2 ** (stage + 1)
+        block = pl.ds((slot // 2**stage) * 2**stage, 2**stage)
+        return pltpu.make_async_remote_copy(
+            src_ref=pairs_ref.at[block],
+            dst_ref=pairs_ref.at[block],
+            send_sem=send_k.at[stage],
+            recv_sem=recv_k.at[stage],
+            device_id={"ctx": me + far - 2 * far * ((me // far) % 2)},
+            device_id_type=pl.DeviceIdType.MESH,
+        )
+
     @pl.when(group == 0)
     def _():
         lax.fori_loop(1, size, greet, 0)
+        for copy in own_copies():
+            copy.start()
 
     def ask(to, origin):
         return pltpu.make_async_remote_copy(
@@ -103,6 +131,16 @@
     @pl.when(group == 0)
     def _():
         pl.semaphore_wait(barrier, size - 1)
+        for copy in own_copies():
+            copy.wait()
+        double(0).start()
+
+    for stage in range(2):
+
+        @pl.when(group == 3 * stage + 3)
+        def _():
+            double(stage).wait()
+            double(stage + 1).start()
 
     filler = jnp.zeros((HEAD - 3 * count, LANES), jnp.float32)
     for part in range(share_count):
@@ -159,6 +197,10 @@
     def _():
         lax.fori_loop(1, size, finish, 0)
         ent_ref[...] = lands[...]
+        for stage in range(2, stages):
+            double(stage).wait()
+            if stage + 1 < stages:
+                double(stage + 1).start()
 
 
 def second_pass(
@@ -195,7 +237,7 @@
         out_ref[:, cols] = (y * silu(gate_ref[:, cols].astype(jnp.float32))).astype(jnp.bfloat16)
 
 
-def attend(place_ref, q_ref, k_ref, v_ref, out_ref):
+def attend(place_ref, at_ref, q_ref, k_ref, v_ref, out_ref):
     rows = q_ref.shape[0]
     keys = k_ref.shape[0]
     heads = q_ref.shape[1] // HEAD_DIM
@@ -209,7 +251,7 @@
             q, k_ref[at, :], (((1,), (1,)), ((), ())), preferred_element_type=jnp.float32
         ).reshape(heads, rows, chunk)
         place = place_ref[0] + lax.broadcasted_iota(jnp.int32, (1, rows, chunk), 1)
-        allowed = first + lax.broadcasted_iota(jnp.int32, (1, rows, chunk), 2) <= place
+        allowed = at_ref[:, at].reshape(1, 1, chunk) <= place
         scores = jnp.where(allowed, scores, -1e30)
         largest = jnp.max(scores, axis=2, keepdims=True)
         if running is not None:
@@ -258,15 +300,13 @@
     size = lax.axis_size("ctx")
     own = lax.axis_index("ctx")
     groups = channels // WIDE
+    stages = size.bit_length() - 1
     tiles = channels // LANES
     f32, bf16 = jnp.float32, jnp.bfloat16
     shape = jax.ShapeDtypeStruct
 
     rim = lax.ppermute(
         mixer_input[rows - (TAPS - 1) :], "ctx", [(i, i + 1) for i in range(size - 1)]
-    )
-    pairs = lax.all_gather(
-        jnp.concatenate([key_heads, value_heads], axis=1), "ctx", axis=0, tiled=True
     )
     rates = -LOG2E * jnp.exp(decay_log)
     rates = rates.reshape(tiles, LANES, STATE).transpose(0, 2, 1).reshape(tiles * STATE, LANES)
@@ -282,7 +322,7 @@
     slab = pl.BlockSpec((None, rows * SUB, LANES), lambda g: (g, 0, 0))
     rate_spec = pl.BlockSpec((SUB * STATE, LANES), lambda g: (g, 0))
     slab_shape = shape((groups, rows * SUB, LANES), f32)
-    step, inner, entering = pl.pallas_call(
+    step, inner, entering, pairs = pl.pallas_call(
         first_pass,
         grid=(groups,),
         in_specs=[
@@ -294,16 +334,20 @@
             rate_spec,
             b_spec,
             pl.BlockSpec((tiles * STATE, LANES), lambda g: (0, 0)),
+            pl.BlockSpec(memory_space=pl.ANY),
+            pl.BlockSpec(memory_space=pl.ANY),
         ],
         out_specs=[
             slab,
             slab,
             pl.BlockSpec((size, share, LANES), lambda g: (0, 0, 0)),
+            pl.BlockSpec(memory_space=pl.ANY),
         ],
         out_shape=[
             slab_shape,
             slab_shape,
             shape((size, share, LANES), bf16),
+            shape((size, rows, 2 * KV_HEADS * HEAD_DIM), bf16),
         ],
         scratch_shapes=[
             pltpu.VMEM((SUB + rows, WIDE), f32),
@@ -313,7 +357,9 @@
             pltpu.VMEM((size, share, LANES), bf16),
             pltpu.VMEM((size, share, LANES), bf16),
         ]
-        + [pltpu.SemaphoreType.DMA((size,))] * 4,
+        + [pltpu.SemaphoreType.DMA((size,))] * 4
+        + [pltpu.SemaphoreType.DMA((stages,))] * 2
+        + [pltpu.SemaphoreType.DMA((2,))],
         compiler_params=pltpu.CompilerParams(collective_id=0, has_side_effects=True),
         cost_estimate=pl.CostEstimate(
             flops=6 * rows * channels * STATE,
@@ -321,16 +367,22 @@
             transcendentals=rows * channels * STATE,
         ),
         name="first_pass",
-    )(rim, mixer_input, step_raw, conv_weight.T, conv_bias[None], rates, bc_rows, rates)
+    )(rim, mixer_input, step_raw, conv_weight.T, conv_bias[None], rates, bc_rows, rates, key_heads, value_heads)
 
     entering = entering.reshape(tiles * STATE, LANES)
     panel = Q_HEADS // KV_HEADS * HEAD_DIM
     keys = rows * size
+    pairs = pairs.reshape(keys, 2 * KV_HEADS * HEAD_DIM)
+    origin = [int(f"{p:0{stages}b}"[::-1], 2) for p in range(size)]
+    key_places = jnp.asarray(
+        (np.array(origin)[:, None] * rows + np.arange(rows)).reshape(1, keys), jnp.int32
+    )
     attention = pl.pallas_call(
         attend,
         grid=(KV_HEADS,),
         in_specs=[
             pl.BlockSpec(memory_space=pltpu.SMEM),
+            pl.BlockSpec((1, keys), lambda g: (0, 0)),
             pl.BlockSpec((rows, panel), lambda g: (0, g)),
             pl.BlockSpec((keys, HEAD_DIM), lambda g: (0, g)),
             pl.BlockSpec((keys, HEAD_DIM), lambda g: (0, KV_HEADS + g)),
@@ -343,7 +395,7 @@
             transcendentals=rows * Q_HEADS * keys,
         ),
         name="attend",
-    )((own * rows).astype(jnp.int32)[None], query_heads, pairs, pairs)
+    )((own * rows).astype(jnp.int32)[None], key_places, query_heads, pairs, pairs)
 
     mixer_output = pl.pallas_call(
         second_pass,

time: 88.1 us -> 83.8 us (0.951)
  the two profiles are of different devices: /device:TPU:19 before, /device:TPU:11 now
where the time goes in v4:
time: 83.8 us; the launch traced here: 83.5 us
  Pallas kernels  74 us (88%)
  starting transfers between devices  3.71 us (4%)
  other arithmetic  2.69 us (3%)
  local copies, waits for them, and re-layouts  2.47 us (3%)
    pallas_call x1, Pallas kernels, per_device(): pl.pallas_call(first_pass, grid=(groups,), in_specs=[pl.BlockSpec((TAPS -...  52.5 us
    pallas_call x1, Pallas kernels, per_device(): pl.pallas_call(second_pass, grid=(groups,), in_specs=[slab, slab, wide, p...  13.4 us
    pallas_call x1, Pallas kernels, per_device(): pl.pallas_call(attend, grid=(KV_HEADS,), in_specs=[pl.BlockSpec(memory_sp...  8.04 us
    ppermute x1, starting transfers between devices, per_device(): lax.ppermute(mixer_input[rows - (TAPS - 1):], 'ctx', [(i, i + 1) for i in...  3.71 us
    reshape x1, other arithmetic, per_device(): rates.reshape(tiles, LANES, STATE).transpose(0, 2, 1)  1.9 us
  transfers between devices with their start and end apart: 1, of which 0 were waited for; matrix products, arithmetic and copies ran while one was open for 3% of the time, Pallas kernels for 0%

profile of v4, /device:TPU:11, one launch (start us, length us, event | category | flops | bytes accessed | tf_op | source)
XLA Modules:
  0.0 83.5 jit_solution(12727682825600623246)
XLA Ops:
  0.6 0.9 %slice.3 = bf16[3,8192]{1,0:T(4,128)(2,1)S(1)} slice(bf16[64,8192]{1,0:T(8,128)(2,1)} %x_ref.1), slice={[61:64], [0:8192]} | slice | bytes 98304 | tf_op jit(solution)/shard_map/slice | solution.py:309
  1.6 3.7 %collective-permute-start = (bf16[3,8192]{1,0:T(4,128)(2,1)S(1)}, bf16[3,8192]{1,0:T(4,128)(2,1)S(1)}, u32[]{:S(2)}, u32[]{:S(2)}) collective-permute-start(bf16[3,8192]{1,0:T(4,128)(2,1)S(1)} %slice.3), channel_id=1, source_target_pairs={{0,1},{1,2},{2,3},{3,4},{4,5},{5,6},{6,7},{7,8},{8,9},{9,10},{10,1... | collective-permute-start | bytes 147464 | tf_op jit(solution)/shard_map/ppermute | solution.py:308
  5.3 1.9 %copy_bitcast_fusion = f32[64,128,16]{1,2,0:T(8,128)} fusion(f32[8192,16]{0,1:T(8,128)} %param.18), kind=kLoop, calls=%fused_computation | loop fusion | flops 131072 | bytes 1048576 | tf_op jit(solution)/shard_map/reshape | solution.py:312
  7.2 0.8 pad_maximum_fusion
  8.0 0.1 copy.17
  8.1 0.1 broadcast_in_dim.14
  8.2 0.0 collective-permute-done.rim_ref
  8.2 0.0 copy-start
  8.2 1.3 %broadcast_in_dim.15.b_ref.c_ref = f32[2048,128]{1,0:T(8,128)} broadcast(f32[2048]{0:T(1024)S(1)} %broadcast_in_dim.14), dimensions={0} | broadcast | bytes 1056768 | tf_op jit(solution)/shard_map/broadcast_in_dim | solution.py:313
  9.5 0.0 copy-done
  9.5 52.5 %first_pass.1 = (f32[8,512,128]{2,1,0:T(8,128)}, f32[8,512,128]{2,1,0:T(8,128)}, bf16[16,64,128]{2,1,0:T(8,128)(2,1)}, bf16[16,64,1024]{2,1,0:T(8,128)(2,1)}) custom-call(bf16[3,8192]{1,0:T(4,128)(2,1)} %copy-done, bf16[64,8192]{1,0:T(8,128)(2,1)} %x_ref.1, bf16[64,8192]{1,0:T(8,128)(2,1)} %raw_ref.1, f32[4,8192]{1,0:T(4,128)} %bitcast.19, ...), custom_call_target="tpu_custom_call" | custom-call | flops 50331648 | bytes 4194304 | tf_op jit(solution)/shard_map/first_pass/pallas_call | solution.py:325
  62.0 8.0 %attend.1 = bf16[64,4096]{1,0:T(8,128)(2,1)} custom-call(s32[1]{0:T(128)} %bitcast.6.place_ref, s32[1,1024]{1,0:T(1,128)} %constant.10.clone.at_ref, bf16[64,4096]{1,0:T(8,128)(2,1)} %q_ref.1, bf16[1024,1024]{1,0:T(8,128)(2,1)} %bitcast.14, bf16[1024,1024]{1,0:T(8,128)(2,1)} %bitcast.15), custom_call_target="tpu_custom_call" | custom-call | flops 1073741824 | bytes 2097152 | tf_op jit(solution)/shard_map/attend/pallas_call | solution.py:380
  70.1 13.4 %second_pass.1 = bf16[64,8192]{1,0:T(8,128)(2,1)} custom-call(f32[8,512,128]{2,1,0:T(8,128)} %get-tuple-element.6.step_ref, f32[8,512,128]{2,1,0:T(8,128)} %get-tuple-element.7.inner_ref, bf16[64,8192]{1,0:T(8,128)(2,1)} %gate_ref.1, f32[64,128]{1,0:T(8,128)} %bitcast.21, f32[1024,128]{1,0:T(8,128)} %bitcast.18, f32[2048,128]{1,0:T(8,128)} %broadcast_in_dim.15.b_ref.c_ref, ...), custom_call_target="tpu_custom_call" | custom-call | flops 67108864 | bytes 6291456 | tf_op jit(solution)/shard_map/second_pass/pallas_call | solution.py:400
Async XLA Ops:
  1.6 6.6 %collective-permute-start = (bf16[3,8192]{1,0:T(4,128)(2,1)S(1)}, bf16[3,8192]{1,0:T(4,128)(2,1)S(1)}, u32[]{:S(2)}, u32[]{:S(2)}) collective-permute-start(bf16[3,8192]{1,0:T(4,128)(2,1)S(1)} %slice.3), channel_id=1, source_target_pairs={{0,1},{1,2},{2,3},{3,4},{4,5},{5,6},{6,7},{7,8},{8,9},{9,10},{10,1... | collective-permute-start | bytes 147464 | tf_op jit(solution)/shard_map/ppermute | solution.py:308
  8.2 1.4 %copy-start = (bf16[3,8192]{1,0:T(4,128)(2,1)}, bf16[3,8192]{1,0:T(4,128)(2,1)S(1)}, u32[]{:S(2)}) copy-start(bf16[3,8192]{1,0:T(4,128)(2,1)S(1)} %collective-permute-done.rim_ref) | copy-start | bytes 147460

commit v5 on v4

--- a/solution.py
+++ b/solution.py
@@ -22,6 +22,36 @@
 
 def silu(v):
     return v / (1.0 + jnp.exp(-v))
+
+
+EARLY = 2
+
+
+def slot_of(size, me):
+    stages = size.bit_length() - 1
+    return sum(((me // 2**b) % 2) * 2 ** (stages - 1 - b) for b in range(stages)), stages
+
+
+def partner(size, stage):
+    me = lax.axis_index("ctx")
+    far = size // 2 ** (stage + 1)
+    return me + far - 2 * far * ((me // far) % 2)
+
+
+def held(size, stage):
+    slot, _ = slot_of(size, lax.axis_index("ctx"))
+    return pl.ds((slot // 2**stage) * 2**stage, 2**stage)
+
+
+def doubling(size, stage, source, target, send, recv):
+    return pltpu.make_async_remote_copy(
+        src_ref=source.at[held(size, stage)],
+        dst_ref=target.at[held(size, stage)],
+        send_sem=send.at[stage],
+        recv_sem=recv.at[stage],
+        device_id={"ctx": partner(size, stage)},
+        device_id_type=pl.DeviceIdType.MESH,
+    )
 
 
 def first_pass(
@@ -47,8 +77,7 @@
         )
         return 0
 
-    stages = size.bit_length() - 1
-    slot = sum(((me // 2**b) % 2) * 2 ** (stages - 1 - b) for b in range(stages))
+    slot, _ = slot_of(size, me)
 
     def own_copies():
         width = key_ref.shape[1]
@@ -60,16 +89,7 @@
         ]
 
     def double(stage):
-        far = size // 2 ** (stage + 1)
-        block = pl.ds((slot // 2**stage) * 2**stage, 2**stage)
-        return pltpu.make_async_remote_copy(
-            src_ref=pairs_ref.at[block],
-            dst_ref=pairs_ref.at[block],
-            send_sem=send_k.at[stage],
-            recv_sem=recv_k.at[stage],
-            device_id={"ctx": me + far - 2 * far * ((me // far) % 2)},
-            device_id_type=pl.DeviceIdType.MESH,
-        )
+        return doubling(size, stage, pairs_ref, pairs_ref, send_k, recv_k)
 
     @pl.when(group == 0)
     def _():
@@ -135,12 +155,10 @@
             copy.wait()
         double(0).start()
 
-    for stage in range(2):
-
-        @pl.when(group == 3 * stage + 3)
-        def _():
-            double(stage).wait()
-            double(stage + 1).start()
+    @pl.when(group == 5)
+    def _():
+        double(0).wait()
+        double(1).start()
 
     filler = jnp.zeros((HEAD - 3 * count, LANES), jnp.float32)
     for part in range(share_count):
@@ -197,16 +215,41 @@
     def _():
         lax.fori_loop(1, size, finish, 0)
         ent_ref[...] = lands[...]
-        for stage in range(2, stages):
-            double(stage).wait()
-            if stage + 1 < stages:
-                double(stage + 1).start()
+        double(1).wait()
 
 
 def second_pass(
-    step_ref, inner_ref, gate_ref, skip_ref, rate_ref, b_ref, c_ref, ent_ref, out_ref, ent, ysc
+    step_ref, inner_ref, gate_ref, skip_ref, rate_ref, b_ref, c_ref, ent_ref, some_ref,
+    out_ref, pairs_ref, ent, ysc, send_k, recv_k, own_k
 ):
     rows = gate_ref.shape[0]
+    size = some_ref.shape[0]
+    group = pl.program_id(0)
+    groups = pl.num_programs(0)
+    stages = size.bit_length() - 1
+    barrier = pltpu.get_barrier_semaphore()
+
+    def carry_over():
+        block = held(size, EARLY)
+        return pltpu.make_async_copy(some_ref.at[block], pairs_ref.at[block], own_k.at[0])
+
+    def double(stage):
+        source = some_ref if stage == EARLY else pairs_ref
+        return doubling(size, stage, source, pairs_ref, send_k, recv_k)
+
+    @pl.when(group == 0)
+    def _():
+        for stage in range(EARLY, stages):
+            pl.semaphore_signal(
+                barrier,
+                inc=1,
+                device_id={"ctx": partner(size, stage)},
+                device_id_type=pl.DeviceIdType.MESH,
+            )
+        carry_over().start()
+        pl.semaphore_wait(barrier, stages - EARLY)
+        double(EARLY).start()
+
     ent[...] = ent_ref[...].astype(jnp.float32)
     rates = [rate_ref[pl.ds(n, SUB, stride=STATE), :] for n in range(STATE)]
     start = tuple(ent[pl.ds(n, SUB, stride=STATE), :] for n in range(STATE))
@@ -235,6 +278,19 @@
         cols = pl.ds(k * LANES, LANES)
         y = ysc[pl.ds(k, rows, stride=SUB), :]
         out_ref[:, cols] = (y * silu(gate_ref[:, cols].astype(jnp.float32))).astype(jnp.bfloat16)
+
+    @pl.when(group == groups - 2)
+    def _():
+        carry_over().wait()
+        double(EARLY).wait()
+        double(EARLY + 1).start()
+
+    @pl.when(group == groups - 1)
+    def _():
+        for stage in range(EARLY + 1, stages):
+            double(stage).wait()
+            if stage + 1 < stages:
+                double(stage + 1).start()
 
 
 def attend(place_ref, at_ref, q_ref, k_ref, v_ref, out_ref):
@@ -322,7 +378,7 @@
     slab = pl.BlockSpec((None, rows * SUB, LANES), lambda g: (g, 0, 0))
     rate_spec = pl.BlockSpec((SUB * STATE, LANES), lambda g: (g, 0))
     slab_shape = shape((groups, rows * SUB, LANES), f32)
-    step, inner, entering, pairs = pl.pallas_call(
+    step, inner, entering, some = pl.pallas_call(
         first_pass,
         grid=(groups,),
         in_specs=[
@@ -370,6 +426,39 @@
     )(rim, mixer_input, step_raw, conv_weight.T, conv_bias[None], rates, bc_rows, rates, key_heads, value_heads)
 
     entering = entering.reshape(tiles * STATE, LANES)
+    mixer_output, pairs = pl.pallas_call(
+        second_pass,
+        grid=(groups,),
+        in_specs=[
+            slab,
+            slab,
+            wide,
+            pl.BlockSpec((SUB, LANES), lambda g: (g, 0)),
+            rate_spec,
+            b_spec,
+            c_spec,
+            rate_spec,
+            pl.BlockSpec(memory_space=pl.ANY),
+        ],
+        out_specs=[wide, pl.BlockSpec(memory_space=pl.ANY)],
+        out_shape=[
+            shape((rows, channels), bf16),
+            shape((size, rows, 2 * KV_HEADS * HEAD_DIM), bf16),
+        ],
+        scratch_shapes=[
+            pltpu.VMEM((SUB * STATE, LANES), f32),
+            pltpu.VMEM((rows * SUB, LANES), f32),
+        ]
+        + [pltpu.SemaphoreType.DMA((stages,))] * 2
+        + [pltpu.SemaphoreType.DMA((1,))],
+        compiler_params=pltpu.CompilerParams(collective_id=1, has_side_effects=True),
+        cost_estimate=pl.CostEstimate(
+            flops=8 * rows * channels * STATE,
+            bytes_accessed=12 * rows * channels,
+            transcendentals=rows * channels * STATE,
+        ),
+        name="second_pass",
+    )(step, inner, gate_input, skip_gain.reshape(tiles, LANES), rates, bc_rows, bc_rows, entering, some)
     panel = Q_HEADS // KV_HEADS * HEAD_DIM
     keys = rows * size
     pairs = pairs.reshape(keys, 2 * KV_HEADS * HEAD_DIM)
@@ -397,32 +486,6 @@
         name="attend",
     )((own * rows).astype(jnp.int32)[None], key_places, query_heads, pairs, pairs)
 
-    mixer_output = pl.pallas_call(
-        second_pass,
-        grid=(groups,),
-        in_specs=[
-            slab,
-            slab,
-            wide,
-            pl.BlockSpec((SUB, LANES), lambda g: (g, 0)),
-            rate_spec,
-            b_spec,
-            c_spec,
-            rate_spec,
-        ],
-        out_specs=wide,
-        out_shape=shape((rows, channels), bf16),
-        scratch_shapes=[
-            pltpu.VMEM((SUB * STATE, LANES), f32),
-            pltpu.VMEM((rows * SUB, LANES), f32),
-        ],
-        cost_estimate=pl.CostEstimate(
-            flops=8 * rows * channels * STATE,
-            bytes_accessed=12 * rows * channels,
-            transcendentals=rows * channels * STATE,
-        ),
-        name="second_pass",
-    )(step, inner, gate_input, skip_gain.reshape(tiles, LANES), rates, bc_rows, bc_rows, entering)
     return (mixer_output, attention)
 
 

time: 83.8 us -> 85.2 us (1.017)
  the two profiles are of different devices: /device:TPU:11 before, /device:TPU:0 now
where the time goes in v5:
time: 85.2 us; the launch traced here: 84.9 us
  Pallas kernels  75.7 us (89%)
  local copies, waits for them, and re-layouts  3.41 us (4%)
  other arithmetic  2.7 us (3%)
  starting transfers between devices  2.36 us (3%)
    pallas_call x1, Pallas kernels, per_device(): pl.pallas_call(first_pass, grid=(groups,), in_specs=[pl.BlockSpec((TAPS -...  45.5 us
    pallas_call x1, Pallas kernels, per_device(): pl.pallas_call(second_pass, grid=(groups,), in_specs=[slab, slab, wide, p...  22.1 us
    pallas_call x1, Pallas kernels, per_device(): pl.pallas_call(attend, grid=(KV_HEADS,), in_specs=[pl.BlockSpec(memory_sp...  8.12 us
    ppermute x1, starting transfers between devices, per_device(): lax.ppermute(mixer_input[rows - (TAPS - 1):], 'ctx', [(i, i + 1) for i in...  2.36 us
    reshape x1, other arithmetic, per_device(): rates.reshape(tiles, LANES, STATE).transpose(0, 2, 1)  1.91 us
  transfers between devices with their start and end apart: 1, of which 0 were waited for; matrix products, arithmetic and copies ran while one was open for 3% of the time, Pallas kernels for 0%

profile of v5, /device:TPU:0, one launch (start us, length us, event | category | flops | bytes accessed | tf_op | source)
XLA Modules:
  0.0 84.9 jit_solution(4591147598152529205)
XLA Ops:
  0.6 0.9 %slice.3 = bf16[3,8192]{1,0:T(4,128)(2,1)S(1)} slice(bf16[64,8192]{1,0:T(8,128)(2,1)} %x_ref.1), slice={[61:64], [0:8192]} | slice | bytes 98304 | tf_op jit(solution)/shard_map/slice | solution.py:365
  1.6 2.4 %collective-permute-start = (bf16[3,8192]{1,0:T(4,128)(2,1)S(1)}, bf16[3,8192]{1,0:T(4,128)(2,1)S(1)}, u32[]{:S(2)}, u32[]{:S(2)}) collective-permute-start(bf16[3,8192]{1,0:T(4,128)(2,1)S(1)} %slice.3), channel_id=1, source_target_pairs={{0,1},{1,2},{2,3},{3,4},{4,5},{5,6},{6,7},{7,8},{8,9},{9,10},{10,1... | collective-permute-start | bytes 147464 | tf_op jit(solution)/shard_map/ppermute | solution.py:364
  3.9 1.9 %copy_bitcast_fusion = f32[64,128,16]{1,2,0:T(8,128)} fusion(f32[8192,16]{0,1:T(8,128)} %param.18), kind=kLoop, calls=%fused_computation | loop fusion | flops 131072 | bytes 1048576 | tf_op jit(solution)/shard_map/reshape | solution.py:368
  5.9 0.8 pad_maximum_fusion
  6.6 0.1 copy.17
  6.7 0.1 broadcast_in_dim.14
  6.8 0.0 collective-permute-done.rim_ref
  6.8 0.0 copy-start.1
  6.8 1.3 %broadcast_in_dim.15.b_ref.c_ref = f32[2048,128]{1,0:T(8,128)} broadcast(f32[2048]{0:T(1024)S(1)} %broadcast_in_dim.14), dimensions={0} | broadcast | bytes 1056768 | tf_op jit(solution)/shard_map/broadcast_in_dim | solution.py:369
  8.2 0.0 copy-done.1
  8.2 45.5 %first_pass.1 = (f32[8,512,128]{2,1,0:T(8,128)}, f32[8,512,128]{2,1,0:T(8,128)}, bf16[16,64,128]{2,1,0:T(8,128)(2,1)}, bf16[16,64,1024]{2,1,0:T(8,128)(2,1)}) custom-call(bf16[3,8192]{1,0:T(4,128)(2,1)} %copy-done.1, bf16[64,8192]{1,0:T(8,128)(2,1)} %x_ref.1, bf16[64,8192]{1,0:T(8,128)(2,1)} %raw_ref.1, f32[4,8192]{1,0:T(4,128)} %bitcast.19, ...), custom_call_target="tpu_custom_call" | custom-call | flops 50331648 | bytes 4194304 | tf_op jit(solution)/shard_map/first_pass/pallas_call | solution.py:381
  53.7 22.1 %second_pass.1 = (bf16[64,8192]{1,0:T(8,128)(2,1)}, bf16[16,64,1024]{2,1,0:T(8,128)(2,1)}) custom-call(f32[8,512,128]{2,1,0:T(8,128)} %get-tuple-element.8.step_ref, f32[8,512,128]{2,1,0:T(8,128)} %get-tuple-element.9.inner_ref, bf16[64,8192]{1,0:T(8,128)(2,1)} %gate_ref.1, f32[64,128]{1,0:T(8,128)} %bitcast.21, f32[1024,128]{1,0:T(8,128)} %bitcast.18, ...), custom_call_target="tpu_custom_call" | custom-call | flops 67108864 | bytes 6291456 | tf_op jit(solution)/shard_map/second_pass/pallas_call | solution.py:429
  75.8 0.0 copy-start
  75.8 8.1 %attend.1 = bf16[64,4096]{1,0:T(8,128)(2,1)} custom-call(s32[1]{0:T(128)} %bitcast.6.place_ref, s32[1,1024]{1,0:T(1,128)} %constant.10.clone.at_ref, bf16[64,4096]{1,0:T(8,128)(2,1)} %q_ref.1, bf16[1024,1024]{1,0:T(8,128)(2,1)} %bitcast.14, bf16[1024,1024]{1,0:T(8,128)(2,1)} %bitcast.15), custom_call_target="tpu_custom_call" | custom-call | flops 1073741824 | bytes 2097152 | tf_op jit(solution)/shard_map/attend/pallas_call | solution.py:469
  83.9 0.0 copy-done
  83.9 1.0 %copy.21 = bf16[64,8192]{1,0:T(8,128)(2,1)} copy(bf16[64,8192]{1,0:T(8,128)(2,1)S(1)} %copy-done) | data formatting | bytes 2097152
Async XLA Ops:
  1.6 5.3 %collective-permute-start = (bf16[3,8192]{1,0:T(4,128)(2,1)S(1)}, bf16[3,8192]{1,0:T(4,128)(2,1)S(1)}, u32[]{:S(2)}, u32[]{:S(2)}) collective-permute-start(bf16[3,8192]{1,0:T(4,128)(2,1)S(1)} %slice.3), channel_id=1, source_target_pairs={{0,1},{1,2},{2,3},{3,4},{4,5},{5,6},{6,7},{7,8},{8,9},{9,10},{10,1... | collective-permute-start | bytes 147464 | tf_op jit(solution)/shard_map/ppermute | solution.py:364
  6.8 1.3 %copy-start.1 = (bf16[3,8192]{1,0:T(4,128)(2,1)}, bf16[3,8192]{1,0:T(4,128)(2,1)S(1)}, u32[]{:S(2)}) copy-start(bf16[3,8192]{1,0:T(4,128)(2,1)S(1)} %collective-permute-done.rim_ref) | copy-start | bytes 147460
  75.8 8.1 %copy-start = (bf16[64,8192]{1,0:T(8,128)(2,1)S(1)}, bf16[64,8192]{1,0:T(8,128)(2,1)}, u32[]{:S(2)}) copy-start(bf16[64,8192]{1,0:T(8,128)(2,1)} %get-tuple-element.16) | copy-start | bytes 3145732

commit v6 on v5

--- a/solution.py
+++ b/solution.py
@@ -155,7 +155,7 @@
             copy.wait()
         double(0).start()
 
-    @pl.when(group == 5)
+    @pl.when(group == groups - 1)
     def _():
         double(0).wait()
         double(1).start()
@@ -198,7 +198,7 @@
 
         return tuple(new)
 
-    @pl.when(group == jnp.minimum(me // share_count + 2, groups - 1))
+    @pl.when(group == groups - 1)
     def _():
         got[me] = snd[me]
         lax.fori_loop(0, size, join, (jnp.zeros((per, LANES), jnp.float32),) * count)

time: 85.2 us -> 78.6 us (0.923)
  Pallas kernels: 75.7 us -> 69.1 us
    pallas_call x1, Pallas kernels: 45.5 us -> 38.9 us  [per_device(): pl.pallas_call(first_pass, grid=(groups,), in_specs=[pl.BlockSpec((TAPS -...]
  transfers between devices with their start and end apart: 1 -> 1, of which waited for: 0 -> 0; matrix products, arithmetic and copies ran while one was open for 3% -> 4% of each run, Pallas kernels for 0% -> 0%
where the time goes in v6:
time: 78.6 us; the launch traced here: 78.3 us
  Pallas kernels  69.1 us (88%)
  local copies, waits for them, and re-layouts  3.41 us (4%)
  other arithmetic  2.7 us (3%)
  starting transfers between devices  2.36 us (3%)
    pallas_call x1, Pallas kernels, per_device(): pl.pallas_call(first_pass, grid=(groups,), in_specs=[pl.BlockSpec((TAPS -...  38.9 us
    pallas_call x1, Pallas kernels, per_device(): pl.pallas_call(second_pass, grid=(groups,), in_specs=[slab, slab, wide, p...  22.1 us
    pallas_call x1, Pallas kernels, per_device(): pl.pallas_call(attend, grid=(KV_HEADS,), in_specs=[pl.BlockSpec(memory_sp...  8.13 us
    ppermute x1, starting transfers between devices, per_device(): lax.ppermute(mixer_input[rows - (TAPS - 1):], 'ctx', [(i, i + 1) for i in...  2.36 us
    reshape x1, other arithmetic, per_device(): rates.reshape(tiles, LANES, STATE).transpose(0, 2, 1)  1.91 us
  transfers between devices with their start and end apart: 1, of which 0 were waited for; matrix products, arithmetic and copies ran while one was open for 4% of the time, Pallas kernels for 0%

profile of v6, /device:TPU:0, one launch (start us, length us, event | category | flops | bytes accessed | tf_op | source)
XLA Modules:
  0.0 78.3 jit_solution(9358834754418378440)
XLA Ops:
  0.6 0.9 %slice.3 = bf16[3,8192]{1,0:T(4,128)(2,1)S(1)} slice(bf16[64,8192]{1,0:T(8,128)(2,1)} %x_ref.1), slice={[61:64], [0:8192]} | slice | bytes 98304 | tf_op jit(solution)/shard_map/slice | solution.py:365
  1.6 2.4 %collective-permute-start = (bf16[3,8192]{1,0:T(4,128)(2,1)S(1)}, bf16[3,8192]{1,0:T(4,128)(2,1)S(1)}, u32[]{:S(2)}, u32[]{:S(2)}) collective-permute-start(bf16[3,8192]{1,0:T(4,128)(2,1)S(1)} %slice.3), channel_id=1, source_target_pairs={{0,1},{1,2},{2,3},{3,4},{4,5},{5,6},{6,7},{7,8},{8,9},{9,10},{10,1... | collective-permute-start | bytes 147464 | tf_op jit(solution)/shard_map/ppermute | solution.py:364
  3.9 1.9 %copy_bitcast_fusion = f32[64,128,16]{1,2,0:T(8,128)} fusion(f32[8192,16]{0,1:T(8,128)} %param.18), kind=kLoop, calls=%fused_computation | loop fusion | flops 131072 | bytes 1048576 | tf_op jit(solution)/shard_map/reshape | solution.py:368
  5.9 0.8 %pad_maximum_fusion = f32[128,16]{0,1:T(8,128)S(1)} fusion(f32[64,16]{0,1:T(8,128)} %param.17, f32[64,16]{0,1:T(8,128)} %param.16), kind=kLoop, calls=%fused_computation.2 | loop fusion | flops 2048 | bytes 16384 | tf_op jit(solution)/shard_map/concatenate | solution.py:370
  6.6 0.1 copy.17
  6.7 0.1 broadcast_in_dim.14
  6.8 0.0 collective-permute-done.rim_ref
  6.8 0.0 copy-start.1
  6.8 1.3 %broadcast_in_dim.15.b_ref.c_ref = f32[2048,128]{1,0:T(8,128)} broadcast(f32[2048]{0:T(1024)S(1)} %broadcast_in_dim.14), dimensions={0} | broadcast | bytes 1056768 | tf_op jit(solution)/shard_map/broadcast_in_dim | solution.py:369
  8.2 0.0 copy-done.1
  8.2 38.9 %first_pass.1 = (f32[8,512,128]{2,1,0:T(8,128)}, f32[8,512,128]{2,1,0:T(8,128)}, bf16[16,64,128]{2,1,0:T(8,128)(2,1)}, bf16[16,64,1024]{2,1,0:T(8,128)(2,1)}) custom-call(bf16[3,8192]{1,0:T(4,128)(2,1)} %copy-done.1, bf16[64,8192]{1,0:T(8,128)(2,1)} %x_ref.1, bf16[64,8192]{1,0:T(8,128)(2,1)} %raw_ref.1, f32[4,8192]{1,0:T(4,128)} %bitcast.19, ...), custom_call_target="tpu_custom_call" | custom-call | flops 50331648 | bytes 4194304 | tf_op jit(solution)/shard_map/first_pass/pallas_call | solution.py:381
  47.0 22.1 %second_pass.1 = (bf16[64,8192]{1,0:T(8,128)(2,1)}, bf16[16,64,1024]{2,1,0:T(8,128)(2,1)}) custom-call(f32[8,512,128]{2,1,0:T(8,128)} %get-tuple-element.8.step_ref, f32[8,512,128]{2,1,0:T(8,128)} %get-tuple-element.9.inner_ref, bf16[64,8192]{1,0:T(8,128)(2,1)} %gate_ref.1, f32[64,128]{1,0:T(8,128)} %bitcast.21, f32[1024,128]{1,0:T(8,128)} %bitcast.18, ...), custom_call_target="tpu_custom_call" | custom-call | flops 67108864 | bytes 6291456 | tf_op jit(solution)/shard_map/second_pass/pallas_call | solution.py:429
  69.2 0.0 copy-start
  69.2 8.1 %attend.1 = bf16[64,4096]{1,0:T(8,128)(2,1)} custom-call(s32[1]{0:T(128)} %bitcast.6.place_ref, s32[1,1024]{1,0:T(1,128)} %constant.10.clone.at_ref, bf16[64,4096]{1,0:T(8,128)(2,1)} %q_ref.1, bf16[1024,1024]{1,0:T(8,128)(2,1)} %bitcast.14, bf16[1024,1024]{1,0:T(8,128)(2,1)} %bitcast.15), custom_call_target="tpu_custom_call" | custom-call | flops 1073741824 | bytes 2097152 | tf_op jit(solution)/shard_map/attend/pallas_call | solution.py:469
  77.3 0.0 copy-done
  77.3 1.0 %copy.21 = bf16[64,8192]{1,0:T(8,128)(2,1)} copy(bf16[64,8192]{1,0:T(8,128)(2,1)S(1)} %copy-done) | data formatting | bytes 2097152
Async XLA Ops:
  1.6 5.3 %collective-permute-start = (bf16[3,8192]{1,0:T(4,128)(2,1)S(1)}, bf16[3,8192]{1,0:T(4,128)(2,1)S(1)}, u32[]{:S(2)}, u32[]{:S(2)}) collective-permute-start(bf16[3,8192]{1,0:T(4,128)(2,1)S(1)} %slice.3), channel_id=1, source_target_pairs={{0,1},{1,2},{2,3},{3,4},{4,5},{5,6},{6,7},{7,8},{8,9},{9,10},{10,1... | collective-permute-start | bytes 147464 | tf_op jit(solution)/shard_map/ppermute | solution.py:364
  6.8 1.3 %copy-start.1 = (bf16[3,8192]{1,0:T(4,128)(2,1)}, bf16[3,8192]{1,0:T(4,128)(2,1)S(1)}, u32[]{:S(2)}) copy-start(bf16[3,8192]{1,0:T(4,128)(2,1)S(1)} %collective-permute-done.rim_ref) | copy-start | bytes 147460
  69.2 8.1 %copy-start = (bf16[64,8192]{1,0:T(8,128)(2,1)S(1)}, bf16[64,8192]{1,0:T(8,128)(2,1)}, u32[]{:S(2)}) copy-start(bf16[64,8192]{1,0:T(8,128)(2,1)} %get-tuple-element.16) | copy-start | bytes 3145732
